TPU v7x, 256 devices: a whole 4x4x8 slice. The times are simulated.
256 devices in a mesh: seq: 32 (over z, x), chan: 8 (over y, core).
Axes of the slice: x: 4, y: 4, z: 8, core: 2. Of those that a mesh axis runs over, the one named last changes fastest.
Arguments:
- token_ids: int32 [8192], P('seq'), may hold values from 0 to 511
- embed_table: bfloat16 [512, 8192], P(None, 'chan'), may hold values from -6 to 6
- se_query: bfloat16 [8192, 8192], P('seq', 'chan'), may hold values from -3 to 3
- se_key: bfloat16 [8192, 8192], P('seq', 'chan'), may hold values from -6 to 6
- se_filter: bfloat16 [512, 7], P('chan'), may hold values from -2 to 2
- mr_query: bfloat16 [8192, 8192], P('seq', 'chan'), may hold values from -3 to 3
- mr_key: bfloat16 [8192, 8192], P('seq', 'chan'), may hold values from -6 to 6
- mr_filter: bfloat16 [512, 128], P('chan'), may hold values from -0.5 to 0.5
- li_query: bfloat16 [8192, 8192], P('seq', 'chan'), may hold values from -3 to 3
- li_key: bfloat16 [8192, 8192], P('seq', 'chan'), may hold values from -6 to 6
- li_rate: float32 [512, 16], P('chan'), may hold values from 1.2207031e-06 to 0.05
- li_residue: float32 [512, 16], P('chan'), may hold values from -1.5 to 1.5
- attn_query: bfloat16 [8192, 8192], P('seq', 'chan'), may hold values from -7 to 7
- attn_key: bfloat16 [8192, 8192], P('seq', 'chan'), may hold values from -7 to 7
Outputs:
- block_out: bfloat16 [8192, 8192], P('seq', 'chan')
All inputs are finite; a program needn't handle non-finite values.
Results may differ from a plain program's by a relative error of at most 0.01.
Values may be sent and summed in bfloat16 or wider, within the bound.
No kernel may reach another device: no remote copies, remote signals or barrier semaphores. Data moves between devices by JAX's collectives and lax.ppermute only.
A program may use at most 192 MiB of HBM per device.

v0:
```python
import jax
import jax.numpy as jnp
from jax import lax
from jax.sharding import PartitionSpec as P

HEAD_DIM = 128


HIGHEST = lax.Precision.HIGHEST


def from_behind(block, axis, distance):
    devices = range(lax.axis_size(axis))
    route = [(i - distance, i) for i in devices if i - distance in devices]
    return lax.ppermute(block, axis, route)


def carried_in(value, axis, combine, identity):
    count, here = (lax.axis_size(axis), lax.axis_index(axis))
    everything = jax.tree.map(lambda part: lax.all_gather(part, axis), value)
    start = jax.tree.map(
        lambda part, zero: jnp.broadcast_to(jnp.asarray(zero, part.dtype), part.shape),
        value,
        identity,
    )

    def step(k, before):
        reached = k < here
        new = combine(before, jax.tree.map(lambda part: part[k], everything))
        return jax.tree.map(lambda a, b: jnp.where(reached, a, b), new, before)

    return lax.fori_loop(0, count, step, start)


def toeplitz_tables(filters, taps):
    lag_grid = (
        jnp.arange(taps, dtype=jnp.int32)[:, None] - jnp.arange(taps, dtype=jnp.int32)[None, :]
    )
    tap_ids = jnp.arange(taps, dtype=jnp.int32)[:, None, None]
    near_select = (lag_grid[None] == tap_ids).astype(jnp.float32)
    far_select = ((lag_grid + taps)[None] == tap_ids).astype(jnp.float32)
    filters_f = filters.astype(jnp.float32)
    current = jnp.einsum("gk,kts->gts", filters_f, near_select, precision=HIGHEST)
    previous = jnp.einsum("gk,kts->gts", filters_f, far_select, precision=HIGHEST)
    return (current, previous)


def local(
    token_ids,
    embed_table,
    se_query,
    se_key,
    se_filter,
    mr_query,
    mr_key,
    mr_filter,
    li_query,
    li_key,
    li_rate,
    li_residue,
    attn_query,
    attn_key,
):
    f32 = jnp.float32
    bf16 = jnp.bfloat16
    row_count = token_ids.shape[0]
    channels = embed_table.shape[1]
    group_count = se_filter.shape[0]
    group_width = channels // group_count
    seq_count = lax.axis_size("seq")
    chan_count = lax.axis_size("chan")
    total_len = row_count * seq_count
    vocab_ids = jnp.arange(embed_table.shape[0], dtype=jnp.int32)
    one_hot = (token_ids[:, None] == vocab_ids[None, :]).astype(bf16)
    stream = jnp.dot(one_hot, embed_table, preferred_element_type=f32).astype(bf16)
    se_taps = se_filter.shape[1]
    se_input = (se_key.astype(f32) * stream.astype(f32)).astype(bf16)
    se_edge = from_behind(se_input[row_count - (se_taps - 1) :], "seq", 1)
    se_padded = jnp.concatenate([se_edge, se_input], 0)
    tap_weights = jnp.repeat(se_filter.astype(f32), group_width, axis=0)
    se_conv = jnp.zeros((row_count, channels), f32)
    for tap_index in range(se_taps):
        start_row = se_taps - 1 - tap_index
        se_conv = (
            se_conv
            + se_padded[start_row : start_row + row_count].astype(f32) * tap_weights[:, tap_index]
        )
    stream = (stream.astype(f32) + se_query.astype(f32) * se_conv).astype(bf16)
    mr_taps = mr_filter.shape[1]
    mr_input = (mr_key.astype(f32) * stream.astype(f32)).astype(bf16)
    mr_edge = from_behind(mr_input[row_count - (mr_taps - 1) :], "seq", 1)
    block_count = row_count // mr_taps
    extended = jnp.concatenate([jnp.zeros((1, channels), bf16), mr_edge, mr_input], 0)
    extended = extended.reshape(block_count + 1, mr_taps, group_count, group_width)
    current_f, previous_f = toeplitz_tables(mr_filter, mr_taps)
    current = current_f.astype(bf16)
    previous = previous_f.astype(bf16)
    mr_conv = jnp.einsum("gts,bsgc->btgc", current, extended[1:], preferred_element_type=f32)
    mr_conv = mr_conv + jnp.einsum(
        "gts,bsgc->btgc", previous, extended[:-1], preferred_element_type=f32
    )
    stream = (
        stream.astype(f32) + mr_query.astype(f32) * mr_conv.reshape(row_count, channels)
    ).astype(bf16)
    li_input = (li_key.astype(f32) * stream.astype(f32)).astype(bf16)
    gain = li_residue * jnp.sqrt(1.0 - jnp.exp(-2.0 * li_rate) + 1.0 / total_len)
    lag_values = jnp.arange(mr_taps, dtype=f32)
    kernel_rows = jnp.sum(gain[:, :, None] * jnp.exp(-li_rate[:, :, None] * lag_values), axis=1)
    intra, unused_far = toeplitz_tables(kernel_rows, mr_taps)
    blocks_f = li_input.astype(f32).reshape(block_count, mr_taps, group_count, group_width)
    local_conv = jnp.einsum("gts,bsgc->btgc", intra, blocks_f, precision=HIGHEST)
    to_end = jnp.exp(-li_rate[:, :, None] * (mr_taps - 1 - lag_values))
    block_states = jnp.einsum("gms,bsgc->bmgc", to_end, blocks_f, precision=HIGHEST)
    block_ids = jnp.arange(block_count, dtype=f32)
    tail_decay = jnp.exp(-li_rate[None] * (mr_taps * (block_count - 1 - block_ids))[:, None, None])
    shard_state = jnp.einsum("bgm,bmgc->mgc", tail_decay, block_states, precision=HIGHEST)
    rate_column = li_rate.T[:, :, None]
    shard_decay = jnp.exp(-rate_column * row_count)

    def combine(earlier, later):
        return (earlier[0] * later[0], earlier[1] * later[0] + later[1])

    prefix = carried_in(
        (shard_decay, shard_state),
        "seq",
        combine,
        (jnp.ones_like(shard_decay), jnp.zeros_like(shard_state)),
    )
    carry_in = prefix[1]
    block_lag = block_ids[:, None] - 1.0 - block_ids[None, :]
    mixing = jnp.exp(
        -li_rate[None, None] * (mr_taps * jnp.maximum(block_lag, 0.0))[:, :, None, None]
    )
    mixing = jnp.where(block_lag[:, :, None, None] >= 0, mixing, 0.0)
    lead_decay = jnp.exp(-li_rate[None] * (mr_taps * block_ids)[:, None, None])
    block_carry = jnp.einsum("bdgm,dmgc->bmgc", mixing, block_states, precision=HIGHEST)
    block_carry = block_carry + jnp.einsum("bgm,mgc->bmgc", lead_decay, carry_in, precision=HIGHEST)
    emit = gain[:, None, :] * jnp.exp(-li_rate[:, None, :] * (lag_values + 1.0)[None, :, None])
    carry_conv = jnp.einsum("gtm,bmgc->btgc", emit, block_carry, precision=HIGHEST)
    li_conv = (local_conv + carry_conv).reshape(row_count, channels)
    stream = (stream.astype(f32) + li_query.astype(f32) * li_conv).astype(bf16)
    head_dim = HEAD_DIM
    local_heads = channels // head_dim
    part_rows = row_count // chan_count
    chan_index = lax.axis_index("chan")
    queries = attn_query.reshape(row_count, local_heads, head_dim)
    keys_local = attn_key.reshape(row_count, local_heads, head_dim)
    values_local = stream.reshape(row_count, local_heads, head_dim)
    q_heads, k_heads, v_heads = (
        lax.all_to_all(
            lax.all_to_all(queries, "chan", split_axis=0, concat_axis=1, tiled=True),
            "seq",
            split_axis=1,
            concat_axis=0,
            tiled=True,
        ),
        lax.all_to_all(
            lax.all_to_all(keys_local, "chan", split_axis=0, concat_axis=1, tiled=True),
            "seq",
            split_axis=1,
            concat_axis=0,
            tiled=True,
        ),
        lax.all_to_all(
            lax.all_to_all(values_local, "chan", split_axis=0, concat_axis=1, tiled=True),
            "seq",
            split_axis=1,
            concat_axis=0,
            tiled=True,
        ),
    )
    k_all, v_all = (
        lax.all_gather(k_heads, "chan", axis=0, tiled=True),
        lax.all_gather(v_heads, "chan", axis=0, tiled=True),
    )
    key_index = jnp.arange(chan_count * seq_count * part_rows, dtype=jnp.int32)
    key_chan = key_index // (seq_count * part_rows)
    key_rest = key_index % (seq_count * part_rows)
    key_pos = key_rest // part_rows * row_count + key_chan * part_rows + key_rest % part_rows
    query_count = q_heads.shape[0]
    head_count = q_heads.shape[1]
    query_index = jnp.arange(query_count, dtype=jnp.int32)
    query_pos = (
        query_index // part_rows * row_count + chan_index * part_rows + query_index % part_rows
    )
    block_rows = 512
    scale = head_dim ** (-0.5)

    def attend_block(packed):
        query_block, pos_block = packed
        scores = jnp.einsum("qhd,khd->hqk", query_block, k_all, preferred_element_type=f32) * scale
        allowed = key_pos[None, :] <= pos_block[:, None]
        scores = jnp.where(allowed[None], scores, -1e30)
        peak = jnp.max(scores, axis=2, keepdims=True)
        weights = jnp.where(allowed[None], jnp.exp(scores - peak), 0.0)
        totals = jnp.sum(weights, axis=2)
        mixed = jnp.einsum("hqk,khd->qhd", weights.astype(bf16), v_all, preferred_element_type=f32)
        return (mixed / totals.T[:, :, None]).astype(bf16)

    attended = lax.map(
        attend_block,
        (
            q_heads.reshape(query_count // block_rows, block_rows, head_count, head_dim),
            query_pos.reshape(query_count // block_rows, block_rows),
        ),
    )
    attended = attended.reshape(query_count, head_count, head_dim)
    returned = lax.all_to_all(
        lax.all_to_all(attended, "seq", split_axis=0, concat_axis=1, tiled=True),
        "chan",
        split_axis=1,
        concat_axis=0,
        tiled=True,
    )
    return (stream.astype(f32) + returned.reshape(row_count, channels).astype(f32)).astype(bf16)


def solution(mesh):
    in_specs = (
        P("seq"),
        P(None, "chan"),
        P("seq", "chan"),
        P("seq", "chan"),
        P("chan", None),
        P("seq", "chan"),
        P("seq", "chan"),
        P("chan", None),
        P("seq", "chan"),
        P("seq", "chan"),
        P("chan", None),
        P("chan", None),
        P("seq", "chan"),
        P("seq", "chan"),
    )
    out_specs = P("seq", "chan")
    return jax.shard_map(local, mesh=mesh, in_specs=in_specs, out_specs=out_specs, check_vma=False)
```

profile of v0, /device:TPU:1, one launch (start us, length us, event | category | flops | bytes accessed | tf_op | source)
XLA Modules:
  0.0 443.6 jit_solution(17486918646308028121)
XLA Ops:
  6.6 1.2 copy-done
  7.8 2.3 fusion.75
  10.9 4.1 collective-permute-start
  16.1 2.9 convert_bitcast_fusion
  18.9 3.4 convert_bitcast_fusion.1
  22.5 1.9 fusion.77
  25.2 3.3 collective-permute-start.1
  28.6 1.3 multiply_exponential_fusion
  31.0 2.3 collective-permute-done.1
  34.6 3.0 fusion.58
  37.6 3.0 fusion.72
  41.8 2.2 fusion.79
  45.0 1.6 copy.137
  46.6 7.9 %fusion.121 = f32[16,64,1,16]{3,2,1,0:T(1,128)S(1)} fusion(f32[2,64,16,1]{0,3,1,2:T(1,128)} %bitcast.206, f32[2,16,64,16]{3,0,2,1:T(2,128)S(1)} %copy.137), kind=kOutput, calls=%fused_computation.166 | convolution fusion | flops 393216 | bytes 204800 | tf_op jit(solution)/shard_map/bgm,bmgc->mgc/dot_general | solution.py:116
  55.5 1.1 copy.180
  56.6 15.4 %all_to_all.132 = bf16[256,8,128]{2,1,0:T(8,128)(2,1)S(1)} all-to-all(bf16[256,8,128]{2,1,0:T(8,128)(2,1)S(1)} %bitcast.203), channel_id=1, replica_groups=mesh['seq'=32,'chan'=8] {'chan'}, dimensions={0} | all-to-all | bytes 1048576 | tf_op jit(solution)/shard_map/all_to_all | solution.py:158
  72.1 1.1 copy.148
  73.3 13.2 %all-to-all-start.3 = ((bf16[32,64,128]{2,0,1:T(8,128)(2,1)}), bf16[32,64,128]{2,0,1:T(8,128)(2,1)S(1)}, u32[]{:S(2)}, u32[]{:S(2)}) async-start(bf16[32,64,128]{2,0,1:T(8,128)(2,1)} %copy.148), calls=%async_computation.3 | async-start | bytes 1048576 | tf_op jit(solution)/shard_map/all_to_all | solution.py:157
  86.6 50.0 %all-gather = f32[512,64]{1,0:T(8,128)S(1)} all-gather(f32[16,64]{1,0:T(8,128)S(1)} %get-tuple-element.230), channel_id=2, replica_groups=mesh['seq'=32,'chan'=8] {'seq'}, dimensions={0}, use_global_device_ids=true | all-gather | bytes 135168 | tf_op jit(solution)/shard_map/all_gather | solution.py:20
  137.0 4.5 %fusion.57 = f32[64,128,128,1]{2,0,1,3:T(8,128)} fusion(s32[128,128]{1,0:T(8,128)S(1)} %iota_subtract_fusion, f32[64,128]{1,0:T(8,128)S(1)} %multiply_reduce_fusion), kind=kOutput, calls=%fused_computation.63 | convolution fusion | flops 1612709888 | bytes 4292608 | tf_op jit(solution)/shard_map/gk,kts->gts/dot_general | solution.py:43
  142.6 33.3 %while.26 = (s32[]{:T(128)}, f32[16,64,16]{1,2,0:T(8,128)S(1)}, s32[]{:T(128)}, f32[32,16,64,1]{2,1,3,0:T(8,128)S(1)}, f32[32,16,64,16]{2,3,1,0:T(8,128)}, /*index=5*/s32[]{:T(128)}, s32[]{:T(128)}) while((s32[]{:T(128)}, f32[16,64,16]{1,2,0:T(8,128)S(1)}, s32[]{:T(128)}, f32[32,16,64,1]{2,1,3,0:T(8,128)S(1)}, ...), condition=%wide.region_2.3_spmd.clone, body=%wide.region_1.2_spmd.clone.sunk | while | flops 65540 | bytes 209001 | solution.py:32
  142.6 1.0 fusion.146
  143.7 1.0 fusion.146
  144.7 1.0 fusion.146
  145.8 1.0 fusion.146
  146.8 1.0 fusion.146
  147.8 1.0 fusion.146
  148.9 1.0 fusion.146
  149.9 1.0 fusion.146
  150.9 1.0 fusion.146
  152.0 1.0 fusion.146
  155.1 1.0 fusion.146
  156.1 1.0 fusion.146
  160.3 1.0 fusion.146
  161.3 1.0 fusion.146
  162.4 1.0 fusion.146
  164.4 1.0 fusion.146
  165.5 1.0 fusion.146
  168.6 1.0 fusion.146
  169.6 1.0 fusion.146
  172.8 1.0 fusion.146
  173.8 1.0 fusion.146
  176.1 8.8 %fusion.68 = f32[2,16,64,16]{3,0,2,1:T(2,128)S(1)} fusion(f32[2,16,64,16]{3,0,2,1:T(2,128)S(1)} %copy.137, pred[2,2]{1,0:T(4,128)(4,1)S(1)} %fusion.115, f32[16,64,2]{2,1,0:T(8,128)S(1)} %copy-done.13, f32[16,64,16]{2,1,0:T(8,128)S(1)} %copy.138, f32[2,2]{1,0:T(2,128)S(1)} %maximum_multiply_fusion, f32[64,16]{0,1:T(8,128)S(1)} %get-tuple-element.231), kind=kOutput, calls=%fused_computation.73 | convolution fusion | flops 860160 | bytes 339988 | tf_op jit(solution)/shard_map/bdgm,dmgc->bmgc/dot_general | solution.py:136
  184.9 2.5 fusion.82
  187.5 5.5 %fusion.65 = f32[2,128,64,16]{1,3,0,2:T(8,128)S(1)} fusion(f32[64,2,16,128]{3,2,1,0:T(8,128)S(1)} %fusion.82, f32[64,128,128,1]{2,0,1,3:T(8,128)S(1)} %copy-done.2, bf16[2,128,64,16]{1,0,3,2:T(2,128)(2,1)S(1)} %reshape.189), kind=kOutput, calls=%fused_computation.71 | convolution fusion | flops 402915328 | bytes 6815744 | tf_op jit(solution)/shard_map/gts,bsgc->btgc/dot_general | solution.py:111
  194.0 1.5 fusion.80
  195.6 20.9 %all_to_all.133 = bf16[256,8,128]{2,1,0:T(8,128)(2,1)S(1)} all-to-all(bf16[256,8,128]{2,1,0:T(8,128)(2,1)S(1)} %bitcast.204), channel_id=1, replica_groups=mesh['seq'=32,'chan'=8] {'chan'}, dimensions={0} | all-to-all | bytes 1048576 | tf_op jit(solution)/shard_map/all_to_all | solution.py:165
  217.0 22.9 %all_to_all.134 = bf16[32,64,128]{2,0,1:T(8,128)(2,1)S(1)} all-to-all(bf16[32,64,128]{2,0,1:T(8,128)(2,1)S(1)} %copy.151), channel_id=1, replica_groups=mesh['seq'=32,'chan'=8] {'seq'}, dimensions={1} | all-to-all | bytes 1048576 | tf_op jit(solution)/shard_map/all_to_all | solution.py:164
  240.9 17.3 %all_to_all.135 = bf16[256,8,128]{2,1,0:T(8,128)(2,1)S(1)} all-to-all(bf16[256,8,128]{2,1,0:T(8,128)(2,1)S(1)} %bitcast.205), channel_id=1, replica_groups=mesh['seq'=32,'chan'=8] {'chan'}, dimensions={0} | all-to-all | bytes 1048576 | tf_op jit(solution)/shard_map/all_to_all | solution.py:151
  258.3 1.1 copy.145
  259.5 3.9 all-to-all-start.1
  263.4 15.3 %all-to-all-done.1 = bf16[32,64,128]{2,0,1:T(8,128)(2,1)S(1)} async-done(((bf16[32,64,128]{2,0,1:T(8,128)(2,1)}), bf16[32,64,128]{2,0,1:T(8,128)(2,1)S(1)}, u32[]{:S(2)}, u32[]{:S(2)}) %all-to-all-start.1) | async-done | bytes 524320 | tf_op jit(solution)/shard_map/all_to_all | solution.py:150
  278.8 118.8 %while.25 = (s32[]{:T(128)}, bf16[2,512,2,128]{3,1,0,2:T(8,128)(2,1)S(1)}, s32[2,512]{1,0:T(2,128)S(1)}, bf16[2,512,2,128]{3,1,0,2:T(8,128)(2,1)S(1)}, bf16[8192...) while((s32[]{:T(128)}, bf16[2,512,2,128]{3,1,0,2:T(8,128)(2,1)S(1)}, ...), condition=%wide.region_6.7_spmd.clone, body=%wide.region_3.6_spmd.clone.sunk | while | flops 4366827520 | bytes 134822000 | solution.py:200
  278.8 15.3 %fusion.142 = f32[2,512,8192]{2,1,0:T(8,128)} fusion(bf16[8192,2,128]{2,0,1:T(8,128)(2,1)} %get-tuple-element.351, bf16[2,512,2,128]{3,1,0,2:T(8,128)(2,1)S(1)} %get-tuple-element.350, s32[]{:T(128)} %get-tuple-element.340), kind=kOutput, calls=%fused_computation.16.clone.1 | convolution fusion | flops 2147483648 | bytes 38010884 | tf_op jit(solution)/shard_map/while/body/eval_jaxpr/qhd,khd->hqk/dot_general | solution.py:191
  294.2 2.6 broadcast_compare_fusion.2
  296.8 33.1 %fusion.144 = (f32[2,512]{1,0:T(2,128)S(1)}, bf16[2,512,8192]{2,1,0:T(8,128)(2,1)}) fusion(f32[2,512,8192]{2,1,0:T(8,128)} %fusion.142, pred[512,8192]{1,0:T(8,128)(4,1)S(1)} %broadcast_compare_fusion.2), kind=kOutput, calls=%fused_computation.164.clone.1 | output fusion | flops 67117056 | bytes 54530048 | tf_op jit(solution)/shard_map/while/body/eval_jaxpr/sub | solution.py:195
  329.9 8.3 %fusion.145 = bf16[2,512,2,128]{3,1,0,2:T(8,128)(2,1)S(1)} fusion(bf16[2,512,2,128]{3,1,0,2:T(8,128)(2,1)S(1)} %get-tuple-element.341, s32[]{:T(128)} %get-tuple-element.340, bf16[8192,2,128]{2,0,1:T(8,128)(2,1)S(1)} %copy-done.18, bf16[2,512,8192]{2,1,0:T(8,128)(2,1)} %get-tuple-element.305, f32[512,2]{0,1:T(2,128)S(1)} %bitcast.221), kind=kOutput, calls=%fused_computation.15.clone.1 | convolution fusion | flops 2147745792 | bytes 21237764 | tf_op jit(solution)/shard_map/while/body/eval_jaxpr/hqk,khd->qhd/dot_general | solution.py:197
  338.3 15.3 %fusion.142 = f32[2,512,8192]{2,1,0:T(8,128)} fusion(bf16[8192,2,128]{2,0,1:T(8,128)(2,1)} %get-tuple-element.351, bf16[2,512,2,128]{3,1,0,2:T(8,128)(2,1)S(1)} %get-tuple-element.350, s32[]{:T(128)} %get-tuple-element.340), kind=kOutput, calls=%fused_computation.16.clone.1 | convolution fusion | flops 2147483648 | bytes 38010884 | tf_op jit(solution)/shard_map/while/body/eval_jaxpr/qhd,khd->hqk/dot_general | solution.py:191
  353.6 2.6 broadcast_compare_fusion.2
  356.2 33.1 %fusion.144 = (f32[2,512]{1,0:T(2,128)S(1)}, bf16[2,512,8192]{2,1,0:T(8,128)(2,1)}) fusion(f32[2,512,8192]{2,1,0:T(8,128)} %fusion.142, pred[512,8192]{1,0:T(8,128)(4,1)S(1)} %broadcast_compare_fusion.2), kind=kOutput, calls=%fused_computation.164.clone.1 | output fusion | flops 67117056 | bytes 54530048 | tf_op jit(solution)/shard_map/while/body/eval_jaxpr/sub | solution.py:195
  389.3 8.3 %fusion.145 = bf16[2,512,2,128]{3,1,0,2:T(8,128)(2,1)S(1)} fusion(bf16[2,512,2,128]{3,1,0,2:T(8,128)(2,1)S(1)} %get-tuple-element.341, s32[]{:T(128)} %get-tuple-element.340, bf16[8192,2,128]{2,0,1:T(8,128)(2,1)S(1)} %copy-done.18, bf16[2,512,8192]{2,1,0:T(8,128)(2,1)} %get-tuple-element.305, f32[512,2]{0,1:T(2,128)S(1)} %bitcast.221), kind=kOutput, calls=%fused_computation.15.clone.1 | convolution fusion | flops 2147745792 | bytes 21237764 | tf_op jit(solution)/shard_map/while/body/eval_jaxpr/hqk,khd->qhd/dot_general | solution.py:197
  398.2 21.2 %all_to_all.136 = bf16[1024,2,128]{2,1,0:T(2,128)(2,1)S(1)} all-to-all(bf16[1024,2,128]{2,1,0:T(2,128)(2,1)S(1)} %copy.155), channel_id=1, replica_groups=mesh['seq'=32,'chan'=8] {'seq'}, dimensions={0} | all-to-all | bytes 1048576 | tf_op jit(solution)/shard_map/all_to_all | solution.py:209
  419.6 15.5 %all_to_all.137 = bf16[32,64,128]{2,0,1:T(8,128)(2,1)S(1)} all-to-all(bf16[32,64,128]{2,0,1:T(8,128)(2,1)S(1)} %bitcast.202), channel_id=1, replica_groups=mesh['seq'=32,'chan'=8] {'chan'}, dimensions={1} | all-to-all | bytes 1048576 | tf_op jit(solution)/shard_map/all_to_all | solution.py:208
  435.8 1.1 fusion.81
  (149 shorter events, 25.5 us)
Async XLA Ops:
  6.5 1.2 copy-start
  6.5 12.4 %copy-start.15 = (bf16[64,128]{1,0:T(8,128)(2,1)S(1)}, bf16[64,128]{1,0:T(8,128)(2,1)}, u32[]{:S(2)}) copy-start(bf16[64,128]{1,0:T(8,128)(2,1)} %param.25) | copy-start | bytes 49156
  6.5 15.8 %copy-start.17 = (f32[64,16]{0,1:T(8,128)S(1)}, f32[64,16]{0,1:T(8,128)}, u32[]{:S(2)}) copy-start(f32[64,16]{0,1:T(8,128)} %param.28) | copy-start | bytes 12292
  6.5 15.8 %copy-start.16 = (f32[64,16]{0,1:T(8,128)S(1)}, f32[64,16]{0,1:T(8,128)}, u32[]{:S(2)}) copy-start(f32[64,16]{0,1:T(8,128)} %param.29) | copy-start | bytes 12292
  6.5 136.1 %all-gather.10.cloned.1.call-start = ((), (), s32[]{:S(2)}) async-start(), calls=%async_computation.10 | async-start | bytes 4325376 | tf_op jit(solution)/shard_map/all_gather | solution.py:20
  10.1 0.8 copy-start.6
  10.9 11.5 %copy-start.7 = (bf16[256,1024]{1,0:T(8,128)(2,1)S(1)}, bf16[256,1024]{1,0:T(8,128)(2,1)}, u32[]{:S(2)}) copy-start(bf16[256,1024]{1,0:T(8,128)(2,1)} %copy-done.6) | copy-start | bytes 1572868
  10.9 11.5 %collective-permute-start = (bf16[6,1024]{1,0:T(8,128)(2,1)S(1)}, bf16[6,1024]{1,0:T(8,128)(2,1)S(1)}, u32[]{:S(2)}, u32[]{:S(2)}) collective-permute-start(bf16[6,1024]{1,0:T(8,128)(2,1)S(1)} %slice.74), channel_id=1, source_target_pairs={{0,8},{8,16},{16,24},{24,32},{32,40},{40,48},{48,56},{56,64},{64,7... | collective-permute-start | bytes 36872 | tf_op jit(solution)/shard_map/ppermute | solution.py:15
  16.0 6.4 %copy-start.9 = (bf16[256,1024]{1,0:T(8,128)(2,1)S(1)}, bf16[256,1024]{1,0:T(8,128)(2,1)}, u32[]{:S(2)}) copy-start(bf16[256,1024]{1,0:T(8,128)(2,1)} %get-tuple-element.235) | copy-start | bytes 1572868
  16.0 6.4 %copy-start.10 = (bf16[256,1024]{1,0:T(8,128)(2,1)S(1)}, bf16[256,1024]{1,0:T(8,128)(2,1)}, u32[]{:S(2)}) copy-start(bf16[256,1024]{1,0:T(8,128)(2,1)} %param.24) | copy-start | bytes 1572868
  16.0 6.4 %copy-start.11 = (bf16[256,1024]{1,0:T(8,128)(2,1)S(1)}, bf16[256,1024]{1,0:T(8,128)(2,1)}, u32[]{:S(2)}) copy-start(bf16[256,1024]{1,0:T(8,128)(2,1)} %param.20) | copy-start | bytes 1572868
  25.2 8.1 %collective-permute-start.1 = (bf16[127,1024]{1,0:T(8,128)(2,1)}, bf16[127,1024]{1,0:T(8,128)(2,1)S(1)}, u32[]{:S(2)}, u32[]{:S(2)}) collective-permute-start(bf16[127,1024]{1,0:T(8,128)(2,1)} %slice.91), channel_id=1, source_target_pairs={{0,8},{8,16},{16,24},{24,32},{32,40},{40,48},{48,56},{56,64},{64,7... | collective-permute-start | bytes 780296 | tf_op jit(solution)/shard_map/ppermute | solution.py:15
  34.6 3.0 copy-start.3
  40.6 1.0 copy-start.8
  40.6 1.2 copy-start.12
  73.3 68.4 %all-to-all-start.3 = ((bf16[32,64,128]{2,0,1:T(8,128)(2,1)}), bf16[32,64,128]{2,0,1:T(8,128)(2,1)S(1)}, u32[]{:S(2)}, u32[]{:S(2)}) async-start(bf16[32,64,128]{2,0,1:T(8,128)(2,1)} %copy.148), calls=%async_computation.3 | async-start | bytes 1048576 | tf_op jit(solution)/shard_map/all_to_all | solution.py:157
  86.5 192.3 %all-gather.6.cloned.1.call-start = ((), (), s32[]{:S(2)}) async-start(), calls=%async_computation.8 | async-start | bytes 4718592 | tf_op jit(solution)/shard_map/all_gather | solution.py:173
  137.0 39.1 %copy-start.13 = (f32[16,64,2]{2,1,0:T(8,128)S(1)}, f32[16,64,2]{2,1,0:T(8,128)}, u32[]{:S(2)}) copy-start(f32[16,64,2]{2,1,0:T(8,128)} %get-tuple-element.233) | copy-start | bytes 24580
  142.5 136.3 %all-gather.8.cloned.1.call-start = ((), (), s32[]{:S(2)}) async-start(), calls=%async_computation.9 | async-start | bytes 4718592 | tf_op jit(solution)/shard_map/all_gather | solution.py:174
  176.1 11.4 %copy-start.2 = (f32[64,128,128,1]{2,0,1,3:T(8,128)S(1)}, f32[64,128,128,1]{2,0,1,3:T(8,128)}, u32[]{:S(2)}) copy-start(f32[64,128,128,1]{2,0,1,3:T(8,128)} %fusion.57) | copy-start | bytes 12582916
  194.0 46.8 %copy-start.14 = (bf16[256,1024]{1,0:T(8,128)(2,1)S(1)}, bf16[256,1024]{1,0:T(8,128)(2,1)}, u32[]{:S(2)}) copy-start(bf16[256,1024]{1,0:T(8,128)(2,1)} %param.30) | copy-start | bytes 1572868
  195.5 62.7 %copy-start.4 = (bf16[256,1024]{1,0:T(8,128)(2,1)}, bf16[256,1024]{1,0:T(8,128)(2,1)S(1)}, u32[]{:S(2)}) copy-start(bf16[256,1024]{1,0:T(8,128)(2,1)S(1)} %fusion.80) | copy-start | bytes 1572868
  259.5 19.2 %all-to-all-start.1 = ((bf16[32,64,128]{2,0,1:T(8,128)(2,1)}), bf16[32,64,128]{2,0,1:T(8,128)(2,1)S(1)}, u32[]{:S(2)}, u32[]{:S(2)}) async-start(bf16[32,64,128]{2,0,1:T(8,128)(2,1)} %copy.145), calls=%async_computation.1 | async-start | bytes 1048576 | tf_op jit(solution)/shard_map/all_to_all | solution.py:150
  296.8 33.1 %copy-start.18 = (bf16[8192,2,128]{2,0,1:T(8,128)(2,1)S(1)}, bf16[8192,2,128]{2,0,1:T(8,128)(2,1)}, u32[]{:S(2)}) copy-start(bf16[8192,2,128]{2,0,1:T(8,128)(2,1)} %get-tuple-element.352) | copy-start | bytes 12582916 | tf_op jit(solution)/shard_map/while
  356.2 33.1 %copy-start.18 = (bf16[8192,2,128]{2,0,1:T(8,128)(2,1)S(1)}, bf16[8192,2,128]{2,0,1:T(8,128)(2,1)}, u32[]{:S(2)}) copy-start(bf16[8192,2,128]{2,0,1:T(8,128)(2,1)} %get-tuple-element.352) | copy-start | bytes 12582916 | tf_op jit(solution)/shard_map/while
  398.2 37.6 %copy-start.5 = (bf16[256,1024]{1,0:T(8,128)(2,1)S(1)}, bf16[256,1024]{1,0:T(8,128)(2,1)}, u32[]{:S(2)}) copy-start(bf16[256,1024]{1,0:T(8,128)(2,1)} %copy-done.4) | copy-start | bytes 1572868
  419.4 17.5 %copy-start.1 = (bf16[512,1024]{1,0:T(8,128)(2,1)S(1)}, bf16[512,1024]{1,0:T(8,128)(2,1)}, u32[]{:S(2)}) copy-start(bf16[512,1024]{1,0:T(8,128)(2,1)} %param.19) | copy-start | bytes 3145732
Sparse Core Ops, SparseCore 0:
  55.6 86.0 all-gather.9
  143.5 40.4 all-gather.5
  240.9 34.1 all-gather.7
where the time goes:
time: 450 us; the launch traced here: 444 us
  blocking collectives  163 us (36%)
  other arithmetic  112 us (25%)
  matrix products  91.9 us (20%)
  starting transfers between devices  24.6 us (5%)
  local copies, waits for them, and re-layouts  19 us (4%)
  waiting for transfers between devices  17.7 us (4%)
  between operations  13.9 us (3%)
    sub x2, other arithmetic, attend_block(): weights = jnp.where(allowed[None], jnp.exp(scores - peak), 0.0)  66.2 us
    all_gather x1, blocking collectives, carried_in(): everything = jax.tree.map(lambda part: lax.all_gather(part, axis), value)  50 us
    select_n x32, other arithmetic, step(): return jax.tree.map(lambda a, b: jnp.where(reached, a, b), new, before)  32.1 us
    dot_general x2, matrix products, attend_block(): jnp.einsum('qhd,khd->hqk', query_block, k_all, preferred_element_type=f32)  30.6 us
    all_to_all x1, blocking collectives, local(): lax.all_to_all(lax.all_to_all(values_local, 'chan', split_axis=0, concat_...  22.9 us
    all_to_all x1, blocking collectives, local(): lax.all_to_all(attended, 'seq', split_axis=0, concat_axis=1, tiled=True)  21.2 us
    all_to_all x1, blocking collectives, local(): lax.all_to_all(values_local, 'chan', split_axis=0, concat_axis=1, tiled=T...  20.9 us
    all_to_all x1, blocking collectives, local(): lax.all_to_all(queries, 'chan', split_axis=0, concat_axis=1, tiled=True)  17.3 us
  transfers between devices with their start and end apart: 7, of which 2 were waited for; matrix products, arithmetic and copies ran while one was open for 16% of the time, Pallas kernels for 0%

commit v1 on v0

v1 whole, which is shorter than its diff:
```python
import jax
import jax.numpy as jnp
from jax import lax
from jax.experimental import pallas as pl
from jax.experimental.pallas import tpu as pltpu
from jax.sharding import PartitionSpec as P


F32 = jnp.float32
BF16 = jnp.bfloat16
HEAD = 128
LANES = 128
STRIPE = 4
FACTOR = HEAD ** (-0.5) * 1.4426950408889634
MIB = 2**20


def lane_groups(rows, lanes, width):
    return (lax.broadcasted_iota(jnp.int32, (rows, lanes), 1) % LANES) // width


def tables_kernel(mr_ref, rate_ref, res_ref, total_len, mr_out, li_out):
    at = pl.program_id(0)
    groups, taps = mr_ref.shape
    modes = rate_ref.shape[1]
    span = 2 * taps
    k_id = lax.broadcasted_iota(jnp.int32, (taps, span), 0)
    s_id = lax.broadcasted_iota(jnp.int32, (taps, span), 1)
    reverse = (s_id == taps - k_id).astype(BF16)
    first = jnp.dot(mr_ref[...], reverse, preferred_element_type=F32)
    rate = rate_ref[...]
    gain = res_ref[...] * jnp.sqrt(1.0 - jnp.exp(-2.0 * rate) + 1.0 / total_len)
    s_row = lax.broadcasted_iota(jnp.int32, (groups, span), 1)
    lag = jnp.where(s_row <= taps, taps - s_row, taps + span - s_row).astype(F32)
    to_end = (span - 1 - s_row).astype(F32)
    rows = jnp.zeros((groups, span), F32)
    for m in range(modes):
        column = rate[:, m : m + 1]
        rows = rows + gain[:, m : m + 1] * jnp.exp(-column * lag)
        li_out[at, groups * taps + m * groups : groups * taps + (m + 1) * groups, :] = jnp.exp(
            -column * to_end
        ).astype(BF16)
    keep = s_id <= k_id + taps
    for g in range(groups):
        wide = jnp.broadcast_to(first[g : g + 1, :], (taps, span))
        wide = pltpu.roll(wide, 0, 1, stride=1, stride_axis=0)
        mr_out[at, g * taps : (g + 1) * taps, :] = wide.astype(BF16)
        wide = jnp.broadcast_to(rows[g : g + 1, :], (taps, span))
        wide = pltpu.roll(wide, 0, 1, stride=1, stride_axis=0)
        li_out[at, g * taps : (g + 1) * taps, :] = jnp.where(keep, wide, 0.0).astype(BF16)


def make_tables(mr_filter, li_rate, li_residue, total_len):
    group_count, taps = mr_filter.shape
    modes = li_rate.shape[1]
    per = 8
    blocks = group_count // per

    def body(mr_ref, rate_ref, res_ref, mr_out, li_out):
        tables_kernel(mr_ref, rate_ref, res_ref, total_len, mr_out, li_out)

    return pl.pallas_call(
        body,
        grid=(blocks,),
        in_specs=[
            pl.BlockSpec((per, taps), lambda i: (i, 0)),
            pl.BlockSpec((per, modes), lambda i: (i, 0)),
            pl.BlockSpec((per, modes), lambda i: (i, 0)),
        ],
        out_specs=[pl.BlockSpec(memory_space=pltpu.VMEM)] * 2,
        out_shape=[
            pltpu.VMEM((blocks, per * taps, 2 * taps), BF16),
            pltpu.VMEM((blocks, per * (taps + modes), 2 * taps), BF16),
        ],
        compiler_params=pltpu.CompilerParams(vmem_limit_bytes=24 * MIB),
        name="tables",
    )(mr_filter, li_rate, li_residue)


def embed(tok, table):
    ids = lax.broadcasted_iota(jnp.int32, (tok.shape[0], table.shape[0]), 1)
    one_hot = (tok == ids).astype(BF16)
    return jnp.dot(one_hot, table, preferred_element_type=F32)


def edge_kernel(tok_ref, table_ref, key_ref, out_ref):
    out_ref[...] = (key_ref[...].astype(F32) * embed(tok_ref[...], table_ref[...])).astype(BF16)


def se_kernel(tok_ref, table_ref, edge_ref, query_ref, key_ref, filt_ref, next_ref, stream_out, input_out, tail_out):
    emb = embed(tok_ref[...], table_ref[...])
    rows = emb.shape[0]
    gated = (key_ref[...].astype(F32) * emb).astype(BF16).astype(F32)
    edge = edge_ref[...].astype(F32)
    halo = edge.shape[0]
    padded = jnp.concatenate([edge, gated], 0)
    weights = filt_ref[...]
    conv = gated * weights[0:1, :]
    for k in range(1, weights.shape[0]):
        conv = conv + padded[halo - k : halo - k + rows] * weights[k : k + 1, :]
    stream = (emb + query_ref[...].astype(F32) * conv).astype(BF16)
    stream_out[...] = stream
    gated = (next_ref[...].astype(F32) * stream.astype(F32)).astype(BF16)
    input_out[...] = gated
    tail_out[...] = gated[rows - tail_out.shape[0] :]


def fold_groups(res, taps, groups, width):
    lane_group = lane_groups(taps, res.shape[1], width)
    total = res[0:taps]
    for g in range(1, groups):
        total = jnp.where(lane_group == g, res[g * taps : (g + 1) * taps], total)
    return total


def conv_kernel(mr_tab, li_tab, in_ref, halo_ref, stream_ref, mrq_ref, lik_ref, liq_ref, out_ref):
    at = pl.program_id(0)
    taps = halo_ref.shape[0]
    groups = mr_tab.shape[1] // taps
    modes = li_tab.shape[1] // groups - taps
    width = LANES // groups
    near, far = in_ref[0:taps, :], in_ref[taps:, :]
    right = jnp.concatenate([near, far], 0)
    pair = jnp.concatenate([jnp.concatenate([halo_ref[...], near], 0), right], 1)
    res = jnp.dot(mr_tab[at], pair, preferred_element_type=F32)
    both = fold_groups(res, taps, groups, width)
    conv = jnp.concatenate([both[:, :LANES], both[:, LANES:]], 0)
    stream = (stream_ref[...].astype(F32) + mrq_ref[...].astype(F32) * conv).astype(BF16)
    stream_f = stream.astype(F32)
    gated = (lik_ref[...].astype(F32) * stream_f).astype(BF16)
    near = gated[0:taps, :]
    pair = jnp.concatenate([jnp.concatenate([jnp.zeros_like(near), near], 0), gated], 1)
    res = jnp.dot(li_tab[at], pair, preferred_element_type=F32)
    both = fold_groups(res, taps, groups, width)
    conv = jnp.concatenate([both[:, :LANES], both[:, LANES:]], 0)
    rows = conv.shape[0]
    out_ref[0, 0:rows, :] = (stream_f + liq_ref[...].astype(F32) * conv).astype(BF16)
    ends = res[groups * taps :, LANES:].reshape(modes, groups, LANES)
    mine = lax.broadcasted_iota(jnp.int32, (modes, groups, LANES), 2) // width
    mine = mine == lax.broadcasted_iota(jnp.int32, (modes, groups, LANES), 1)
    state = jnp.sum(jnp.where(mine, ends, 0.0), axis=1)
    high = state.astype(BF16)
    out_ref[0, rows : rows + modes, :] = high
    out_ref[0, rows + modes : rows + 2 * modes, :] = (state - high.astype(F32)).astype(BF16)


def pack_kernel(a_ref, b_ref, c_ref, out_ref):
    rows = a_ref.shape[0]
    for j in range(out_ref.shape[0]):
        for n, ref in enumerate((a_ref, b_ref, c_ref)):
            out_ref[j, n * rows : (n + 1) * rows, :] = ref[:, j * HEAD : (j + 1) * HEAD]


def value_kernel(where_ref, pack_ref, all_ref, liq_ref, s1_ref, s2_ref, s3_ref, rate_ref, res_ref,
                 total_len, out_ref, emit, carry):
    i = pl.program_id(0)
    blocks = all_ref.shape[0]
    rows = out_ref.shape[1]
    modes = rate_ref.shape[0]

    @pl.when(i == 0)
    def _():
        x = where_ref[1]
        rate = rate_ref[...]
        gain = res_ref[...] * jnp.sqrt(1.0 - jnp.exp(-2.0 * rate) + 1.0 / total_len)
        step = (lax.broadcasted_iota(jnp.int32, (rows, LANES), 0) + 1).astype(F32)
        for m in range(modes):
            emit[m] = gain[m : m + 1, :] * jnp.exp(-rate[m : m + 1, :] * step)
        decays = [jnp.exp(-rate * (rows * k)) for k in range(STRIPE + 1)]
        scans = []
        for part in (all_ref, s1_ref, s2_ref, s3_ref):
            running = jnp.zeros((modes, LANES), F32)
            seen = [running]
            for b in range(blocks):
                here = part[b, 0:modes, :].astype(F32) + part[b, modes : 2 * modes, :].astype(F32)
                running = running * decays[STRIPE] + here
                seen.append(running)
            scans.append(seen)
        for b in range(blocks):
            total = decays[STRIPE - 1] * scans[0][b]
            for k in range(1, STRIPE):
                total = total + decays[k - 1] * jnp.where(x >= k, scans[k][b + 1], scans[k][b])
            carry[b] = total

    conv = jnp.zeros((rows, LANES), F32)
    for m in range(modes):
        conv = conv + emit[m] * carry[i, m : m + 1, :]
    value = (pack_ref[0].astype(F32) + liq_ref[0].astype(F32) * conv).astype(BF16)
    out_ref[0] = value


def causal(scores, x, k, rows):
    head = scores[:rows]
    if k == 0:
        row = lax.broadcasted_iota(jnp.int32, head.shape, 0)
        col = lax.broadcasted_iota(jnp.int32, head.shape, 1)
        head = jnp.where(col <= row, head, -1e30)
    else:
        head = jnp.where(x >= k, head, -1e30)
    if scores.shape[0] == rows:
        return head
    return jnp.concatenate([head, scores[rows:]], 0)


def products(where_ref, q_ref, refs, use):
    depth, rows, _ = q_ref.shape
    x = where_ref[1]
    for g in range(depth):
        query = q_ref[g:].reshape((depth - g) * rows, HEAD)
        for n, (k, first, ref) in enumerate(refs):
            if first <= g < first + ref.shape[0]:
                scores = lax.dot_general(
                    query, ref[g - first], (((1,), (1,)), ((), ())), preferred_element_type=F32
                )
                use(g, n, causal(scores, x, k, rows))


def peak_kernel(where_ref, q_ref, k0, k1, k2, k3, k4, peak_out, top_ref):
    depth, rows, _ = q_ref.shape
    top_ref[...] = jnp.full(top_ref.shape, -1e30, F32)

    def use(g, n, scores):
        top = jnp.maximum(scores[:, :LANES], scores[:, LANES:])
        top_ref[g * rows :] = jnp.maximum(top_ref[g * rows :], top)

    half = depth // 2
    refs = ((0, 0, k0), (1, 0, k1), (2, 0, k2), (2, half, k3), (3, 0, k4))
    products(where_ref, q_ref, refs, use)
    for i in range(depth):
        part = jnp.max(top_ref[i * rows : (i + 1) * rows], axis=1, keepdims=True)
        peak_out[i * rows : (i + 1) * rows] = jnp.broadcast_to(part * FACTOR, (rows, LANES))


def gather_up(where_ref, q_ref, peak_ref, refs, values, acc_ref, sum_ref):
    rows = q_ref.shape[1]

    def use(g, n, scores):
        shift = peak_ref[g * rows :]
        low = jnp.exp2(scores[:, :LANES] * FACTOR - shift)
        high = jnp.exp2(scores[:, LANES:] * FACTOR - shift)
        sum_ref[g * rows :] = sum_ref[g * rows :] + (low + high)
        weights = jnp.concatenate([low.astype(BF16), high.astype(BF16)], 1)
        value = values[n][g - refs[n][1]]
        mixed = jnp.dot(weights, value, preferred_element_type=F32)
        acc_ref[g * rows :] = acc_ref[g * rows :] + mixed

    products(where_ref, q_ref, refs, use)


def near_kernel(where_ref, q_ref, peak_ref, k0, k1, k4, v0, v1, v4, acc_ref, sum_ref):
    acc_ref[...] = jnp.zeros(acc_ref.shape, F32)
    sum_ref[...] = jnp.zeros(sum_ref.shape, F32)
    refs = ((0, 0, k0), (1, 0, k1), (3, 0, k4))
    gather_up(where_ref, q_ref, peak_ref, refs, (v0, v1, v4), acc_ref, sum_ref)


def far_kernel(where_ref, q_ref, peak_ref, k2, k3, v2, v3, v0, acc_in, sum_in, out_ref, acc_ref, sum_ref):
    depth, rows, _ = q_ref.shape
    acc_ref[...] = acc_in[...]
    sum_ref[...] = sum_in[...]
    refs = ((2, 0, k2), (2, depth // 2, k3))
    gather_up(where_ref, q_ref, peak_ref, refs, (v2, v3), acc_ref, sum_ref)
    for i in range(depth):
        place = slice(i * rows, (i + 1) * rows)
        total = jnp.sum(sum_ref[place], axis=1, keepdims=True)
        attended = (acc_ref[place] / total).astype(BF16)
        out_ref[i] = (v0[i].astype(F32) + attended.astype(F32)).astype(BF16)


def whole(shape):
    return pl.BlockSpec(shape, lambda *_: (0,) * len(shape))


def local(
    token_ids,
    embed_table,
    se_query,
    se_key,
    se_filter,
    mr_query,
    mr_key,
    mr_filter,
    li_query,
    li_key,
    li_rate,
    li_residue,
    attn_query,
    attn_key,
):
    rows = token_ids.shape[0]
    vocab, channels = embed_table.shape
    group_count = se_filter.shape[0]
    width = channels // group_count
    seq = lax.axis_size("seq")
    total_len = rows * seq
    heads = channels // HEAD
    depth = seq // STRIPE
    taps = mr_filter.shape[1]
    modes = li_rate.shape[1]
    here = lax.axis_index("seq")
    where = jnp.stack([here // STRIPE, here % STRIPE]).astype(jnp.int32)
    smem = pl.BlockSpec(memory_space=pltpu.SMEM)
    columns = [[z * STRIPE + x for z in range(depth)] for x in range(STRIPE)]
    forward = [(d, d + 1) for d in range(seq - 1)]

    def turn(shift):
        return [(d, d // STRIPE * STRIPE + (d + shift) % STRIPE) for d in range(seq)]

    def exchange(packed):
        return lax.all_to_all(
            packed, "seq", split_axis=0, concat_axis=0, tiled=True, axis_index_groups=columns
        )

    def spread(part):
        behind = lax.ppermute(part, "seq", turn(1))
        ahead = lax.ppermute(part, "seq", turn(STRIPE - 1))
        half = depth // 2
        across = [
            lax.ppermute(behind[:half], "seq", turn(1)),
            lax.ppermute(ahead[half:], "seq", turn(STRIPE - 1)),
        ]
        return part, behind, *across, ahead

    early = pl.pallas_call(
        pack_kernel,
        grid=(2,),
        in_specs=[pl.BlockSpec((rows, channels // 2), lambda j: (0, j))] * 3,
        out_specs=pl.BlockSpec((heads // 2, 3 * rows, HEAD), lambda j: (j, 0, 0)),
        out_shape=jax.ShapeDtypeStruct((heads, 3 * rows, HEAD), BF16),
        name="pack",
    )(attn_query, attn_key, li_query)

    tok = token_ids[:, None]
    halo = 8
    last = rows // halo - 1
    edge = pl.pallas_call(
        edge_kernel,
        grid=(1,),
        in_specs=[
            pl.BlockSpec((halo, 1), lambda i: (last, 0)),
            whole((vocab, channels)),
            pl.BlockSpec((halo, channels), lambda i: (last, 0)),
        ],
        out_specs=whole((halo, channels)),
        out_shape=jax.ShapeDtypeStruct((halo, channels), BF16),
        name="edge",
    )(tok, embed_table, se_key)
    edge = lax.ppermute(edge, "seq", forward)

    mr_tab, li_tab = make_tables(mr_filter, li_rate, li_residue, total_len)

    se_taps = se_filter.shape[1]
    se_weights = jnp.broadcast_to(
        se_filter.astype(F32).T[:, :, None], (se_taps, group_count, width)
    ).reshape(se_taps, channels)
    wide = 256
    column = pl.BlockSpec((rows, wide), lambda j: (0, j))
    stream, mr_input, mr_tail = pl.pallas_call(
        se_kernel,
        grid=(channels // wide,),
        in_specs=[
            whole((rows, 1)),
            pl.BlockSpec((vocab, wide), lambda j: (0, j)),
            pl.BlockSpec((halo, wide), lambda j: (0, j)),
            column,
            column,
            pl.BlockSpec((se_taps, wide), lambda j: (0, j)),
            column,
        ],
        out_specs=[column, column, pl.BlockSpec((taps, wide), lambda j: (0, j))],
        out_shape=[jax.ShapeDtypeStruct((rows, channels), BF16)] * 2
        + [jax.ShapeDtypeStruct((taps, channels), BF16)],
        name="short",
    )(tok, embed_table, edge, se_query, se_key, se_weights, mr_key)
    mr_edge = lax.ppermute(mr_tail, "seq", forward)
    early, mr_input = lax.optimization_barrier((early, mr_input))
    early = exchange(early)

    column = pl.BlockSpec((rows, LANES), lambda j: (0, j))
    packed = pl.pallas_call(
        conv_kernel,
        grid=(heads,),
        in_specs=[
            pl.BlockSpec(memory_space=pltpu.VMEM),
            pl.BlockSpec(memory_space=pltpu.VMEM),
            column,
            pl.BlockSpec((taps, LANES), lambda j: (0, j)),
            column,
            column,
            column,
            column,
        ],
        out_specs=pl.BlockSpec((1, rows + 2 * modes, LANES), lambda j: (j, 0, 0)),
        out_shape=jax.ShapeDtypeStruct((heads, rows + 2 * modes, LANES), BF16),
        compiler_params=pltpu.CompilerParams(vmem_limit_bytes=24 * MIB),
        name="medium_long",
    )(mr_tab, li_tab, mr_input, mr_edge, stream, mr_query, li_key, li_query)
    packed = exchange(packed)

    query = early[:, :rows]
    keys = spread(early[:, rows : 2 * rows])
    states = packed[:, rows:]
    others = [lax.ppermute(states, "seq", turn(k)) for k in range(1, STRIPE)]

    def per_channel(value):
        value = jnp.broadcast_to(value.T[:, :, None], (modes, group_count, width))
        return value.reshape(modes, channels)

    def mine(value):
        return lax.dynamic_slice_in_dim(per_channel(value), where[0] * HEAD, HEAD, axis=1)

    def value_body(*refs):
        value_kernel(*refs[:9], total_len, *refs[9:])

    state_spec = whole((depth, 2 * modes, LANES))
    block = pl.BlockSpec((1, rows, LANES), lambda i: (i, 0, 0))
    values = pl.pallas_call(
        value_body,
        grid=(depth,),
        in_specs=[
            smem,
            block,
            state_spec,
            pl.BlockSpec((1, rows, LANES), lambda i: (i, 2, 0)),
            state_spec,
            state_spec,
            state_spec,
            whole((modes, LANES)),
            whole((modes, LANES)),
        ],
        out_specs=block,
        out_shape=jax.ShapeDtypeStruct((depth, rows, LANES), BF16),
        scratch_shapes=[
            pltpu.VMEM((modes, rows, LANES), F32),
            pltpu.VMEM((depth, modes, LANES), F32),
        ],
        name="values",
    )(where, packed, states, early, *others, mine(li_rate), mine(li_residue))
    values = spread(values)

    inside = pl.BlockSpec(memory_space=pltpu.VMEM)
    reach = depth * rows
    peaks = pl.pallas_call(
        peak_kernel,
        in_specs=[smem] + [inside] * 6,
        out_specs=inside,
        out_shape=jax.ShapeDtypeStruct((reach, LANES), F32),
        scratch_shapes=[pltpu.VMEM((reach, LANES), F32)],
        compiler_params=pltpu.CompilerParams(vmem_limit_bytes=30 * MIB),
        name="peaks",
    )(where, query, *keys)
    k0, k1, k2, k3, k4 = keys
    v0, v1, v2, v3, v4 = values
    sums = jax.ShapeDtypeStruct((reach, LANES), F32)
    near = pl.pallas_call(
        near_kernel,
        in_specs=[smem] + [inside] * 8,
        out_specs=[inside, inside],
        out_shape=[sums, sums],
        compiler_params=pltpu.CompilerParams(vmem_limit_bytes=40 * MIB),
        name="near",
    )(where, query, peaks, k0, k1, k4, v0, v1, v4)
    result = pl.pallas_call(
        far_kernel,
        in_specs=[smem] + [inside] * 9,
        out_specs=inside,
        out_shape=jax.ShapeDtypeStruct((depth, rows, HEAD), BF16),
        scratch_shapes=[pltpu.VMEM((reach, HEAD), F32), pltpu.VMEM((reach, LANES), F32)],
        compiler_params=pltpu.CompilerParams(vmem_limit_bytes=40 * MIB),
        name="far",
    )(where, query, peaks, k2, k3, v2, v3, v0, *near)
    result = exchange(result)
    return result.transpose(1, 0, 2).reshape(rows, channels)


def solution(mesh):
    wide = P("seq", "chan")
    narrow = P("chan", None)
    in_specs = (
        P("seq"), P(None, "chan"), wide, wide, narrow, wide, wide, narrow, wide, wide, narrow,
        narrow, wide, wide,
    )

    return jax.shard_map(local, mesh=mesh, in_specs=in_specs, out_specs=wide, check_vma=False)
```

time: 450 us -> 173 us (0.38)
  the two profiles are of different devices: /device:TPU:1 before, /device:TPU:22 now
where the time goes in v1:
time: 173 us
  waiting for transfers between devices  45.3 us (26%)
  Pallas kernels  45.1 us (26%)
  blocking collectives  41.9 us (24%)
  starting transfers between devices  31.4 us (18%)
  local copies, waits for them, and re-layouts  7.77 us (4%)
    all_to_all x2, blocking collectives, exchange(): lax.all_to_all(packed, 'seq', split_axis=0, concat_axis=0, tiled=True, ax...  41.9 us
    all_to_all x1, waiting for transfers between devices, exchange(): lax.all_to_all(packed, 'seq', split_axis=0, concat_axis=0, tiled=True, ax...  30.4 us
    ppermute x2, waiting for transfers between devices, spread(): behind = lax.ppermute(part, 'seq', turn(1))  8.76 us
    pallas_call x1, Pallas kernels, local(): pl.pallas_call(near_kernel, in_specs=[smem] + [inside] * 8, out_specs=[in...  8.5 us
    pallas_call x1, Pallas kernels, local(): pl.pallas_call(conv_kernel, grid=(heads,), in_specs=[pl.BlockSpec(memory_...  7.89 us
    ppermute x2, starting transfers between devices, spread(): lax.ppermute(behind[:half], 'seq', turn(1))  7.4 us
    ppermute x2, starting transfers between devices, spread(): behind = lax.ppermute(part, 'seq', turn(1))  6.46 us
    pallas_call x1, Pallas kernels, local(): pl.pallas_call(value_body, grid=(depth,), in_specs=[smem, block, state_sp...  6.1 us
  transfers between devices with their start and end apart: 14, of which 5 were waited for; matrix products, arithmetic and copies ran while one was open for 2% of the time, Pallas kernels for 16%

profile of v1, /device:TPU:22, one launch (start us, length us, event | category | flops | bytes accessed | tf_op | source)
XLA Modules:
  0.0 172.6 jit_solution(16444709054384593405)
XLA Ops:
  0.0 1.5 copy.18.tok_ref
  1.5 2.1 %edge.1 = bf16[8,1024]{1,0:T(8,128)(2,1)} custom-call(s32[256,1]{1,0:T(8,128)} %copy.18.tok_ref, bf16[512,1024]{1,0:T(8,128)(2,1)} %table_ref.3, bf16[256,1024]{1,0:T(8,128)(2,1)} %key_ref.3), custom_call_target="tpu_custom_call" | custom-call | tf_op jit(solution)/shard_map/edge/pallas_call | solution.py:336
  3.6 3.7 %collective-permute-start = (bf16[8,1024]{1,0:T(8,128)(2,1)}, bf16[8,1024]{1,0:T(8,128)(2,1)S(1)}, u32[]{:S(2)}, u32[]{:S(2)}) collective-permute-start(bf16[8,1024]{1,0:T(8,128)(2,1)} %edge.1), channel_id=1, source_target_pairs={{0,8},{8,16},{16,24},{24,32},{32,40},{40,48},{48,56},{56,64},{64,7... | collective-permute-start | bytes 49160 | tf_op jit(solution)/shard_map/ppermute | solution.py:348
  7.4 0.1 broadcast_in_dim.9
  7.5 0.0 copy-start.14
  7.5 0.0 copy-start.15
  7.5 0.7 reshape.15.filt_ref
  8.2 1.2 collective-permute-done.edge_ref
  9.4 0.6 copy-done.16
  10.0 5.0 %short.1 = (bf16[256,1024]{1,0:T(8,128)(2,1)}, bf16[256,1024]{1,0:T(8,128)(2,1)}, bf16[128,1024]{1,0:T(8,128)(2,1)}) custom-call(s32[256,1]{1,0:T(8,128)} %copy.18.tok_ref, bf16[512,1024]{1,0:T(8,128)(2,1)} %table_ref.3, bf16[8,1024]{1,0:T(8,128)(2,1)} %copy-done.16, bf16[256,1024]{1,0:T(8,128)(2,1)} %query_ref.1, bf16[256,1024]{1,0:T(8,128)(2,1)} %key_ref.3, ...), custom_call_target="tpu_custom_call" | custom-call | tf_op jit(solution)/shard_map/short/pallas_call | solution.py:358
  15.1 5.8 %collective-permute-start.5 = (bf16[128,1024]{1,0:T(8,128)(2,1)}, bf16[128,1024]{1,0:T(8,128)(2,1)S(1)}, u32[]{:S(2)}, u32[]{:S(2)}) collective-permute-start(bf16[128,1024]{1,0:T(8,128)(2,1)} %get-tuple-element.19), channel_id=1, source_target_pairs={{0,8},{8,16},{16,24},{24,32},{32,40},{40,48},{48,56},{56,64},{64,7... | collective-permute-start | bytes 786440 | tf_op jit(solution)/shard_map/ppermute | solution.py:375
  20.9 0.1 copy.19.rate_ref
  21.0 0.1 copy.20.res_ref
  21.1 0.0 copy-start.1
  21.1 0.0 copy-start.2
  21.1 0.0 copy-start.3
  21.1 0.0 copy-start.4
  21.1 2.6 %pack.1 = bf16[8,768,128]{2,1,0:T(8,128)(2,1)} custom-call(bf16[256,1024]{1,0:T(8,128)(2,1)} %a_ref.1, bf16[256,1024]{1,0:T(8,128)(2,1)} %b_ref.1, bf16[256,1024]{1,0:T(8,128)(2,1)} %liq_ref.1), custom_call_target="tpu_custom_call" | custom-call | tf_op jit(solution)/shard_map/pack/pallas_call | solution.py:324
  23.7 3.9 %tables.1 = (bf16[8,1024,256]{2,1,0:T(8,128)(2,1)S(1)}, bf16[8,1152,256]{2,1,0:T(8,128)(2,1)S(1)}) custom-call(bf16[64,128]{1,0:T(8,128)(2,1)S(1)} %copy-done.6, f32[64,16]{1,0:T(8,128)S(1)} %copy.19.rate_ref, f32[64,16]{1,0:T(8,128)S(1)} %copy.20.res_ref), custom_call_target="tpu_custom_call" | custom-call | tf_op jit(solution)/shard_map/tables/pallas_call | solution.py:62
  27.7 0.0 collective-permute-done.5.halo_ref
  27.7 7.9 %medium_long.1 = bf16[8,288,128]{2,1,0:T(8,128)(2,1)S(1)} custom-call(bf16[8,1024,256]{2,1,0:T(8,128)(2,1)S(1)} %get-tuple-element.16.mr_tab, bf16[8,1152,256]{2,1,0:T(8,128)(2,1)S(1)} %get-tuple-element.17.li_tab, bf16[256,1024]{1,0:T(8,128)(2,1)S(1)} %copy-done.5, bf16[128,1024]{1,0:T(8,128)(2,1)S(1)} %collective-permute-done.5.halo_ref, ...), custom_call_target="tpu_custom_call" | custom-call | tf_op jit(solution)/shard_map/medium_long/pallas_call | solution.py:380
  35.6 25.6 %all_to_all.15.refs_1_ = bf16[8,288,128]{2,1,0:T(8,128)(2,1)S(1)} all-to-all(bf16[8,288,128]{2,1,0:T(8,128)(2,1)S(1)} %medium_long.1), channel_id=1, replica_groups={{0,32,64,96,128,160,192,224},{8,40,72,104,136,168,200,232},{16,48,80,11..., dimensions={0} | all-to-all | bytes 1179648 | tf_op jit(solution)/shard_map/all_to_all | solution.py:310
  61.2 3.6 %all-to-all-start = ((bf16[8,768,128]{2,1,0:T(8,128)(2,1)}), bf16[8,768,128]{2,1,0:T(8,128)(2,1)S(1)}, u32[]{:S(2)}, u32[]{:S(2)}) async-start(bf16[8,768,128]{2,1,0:T(8,128)(2,1)} %pack.1), calls=%async_computation | async-start | bytes 3145728 | tf_op jit(solution)/shard_map/all_to_all | solution.py:310
  64.8 0.2 broadcast_in_dim.10
  65.0 0.3 reshape.16
  65.3 0.2 broadcast_in_dim.11
  65.5 0.3 reshape.17
  65.8 0.6 pad_add_fusion.where_ref.refs_0_
  66.4 0.6 constant_dynamic-slice_fusion
  67.0 3.1 %collective-permute-start.6 = (bf16[8,32,128]{2,1,0:T(8,128)(2,1)S(1)}, bf16[8,32,128]{2,1,0:T(8,128)(2,1)S(1)}, u32[]{:S(2)}, u32[]{:S(2)}) collective-permute-start(bf16[8,32,128]{2,1,0:T(8,128)(2,1)S(1)} %slice.32.refs_2_), channel_id=1, source_target_pairs={{0,8},{8,16},{16,24},{24,0},{32,40},{40,48},{48,56},{56,32},{64,72... | collective-permute-start | bytes 196616 | tf_op jit(solution)/shard_map/ppermute | solution.py:403
  70.1 0.0 collective-permute-start.7
  70.1 1.0 collective-permute-start.8
  71.1 30.4 %all-to-all-done.refs_3_ = bf16[8,768,128]{2,1,0:T(8,128)(2,1)S(1)} async-done(((bf16[8,768,128]{2,1,0:T(8,128)(2,1)}), bf16[8,768,128]{2,1,0:T(8,128)(2,1)S(1)}, u32[]{:S(2)}, u32[]{:S(2)}) %all-to-all-start) | async-done | bytes 1572896 | tf_op jit(solution)/shard_map/all_to_all | solution.py:310
  101.5 0.1 fusion
  101.6 1.1 copy-done.8
  102.7 3.2 %collective-permute-start.1 = (bf16[8,256,128]{2,1,0:T(8,128)(2,1)S(1)}, bf16[8,256,128]{2,1,0:T(8,128)(2,1)S(1)}, u32[]{:S(2)}, u32[]{:S(2)}) collective-permute-start(bf16[8,256,128]{2,1,0:T(8,128)(2,1)S(1)} %get-tuple-element.23.k0), channel_id=1, source_target_pairs={{0,8},{8,16},{16,24},{24,0},{32,40},{40,48},{48,56},{56,32},{64,72... | collective-permute-start | bytes 1572872 | tf_op jit(solution)/shard_map/ppermute | solution.py:315
  105.9 0.0 collective-permute-start.3
  105.9 0.0 collective-permute-done.6.refs_4_
  105.9 0.0 collective-permute-done.7.refs_5_
  106.0 0.0 collective-permute-done.8.refs_6_
  106.0 0.6 copy-done.11
  106.5 0.0 copy-done.12
  106.6 0.0 copy-done.13
  106.6 6.1 %values.1.v0 = bf16[8,256,128]{2,1,0:T(8,128)(2,1)} custom-call(s32[2]{0:T(128)} %pad_add_fusion.where_ref.refs_0_, bf16[8,288,128]{2,1,0:T(8,128)(2,1)} %copy-done.9, bf16[8,32,128]{2,1,0:T(8,128)(2,1)} %copy-done.10, bf16[8,768,128]{2,1,0:T(8,128)(2,1)} %copy-done.8, bf16[8,32,128]{2,1,0:T(8,128)(2,1)} %copy-done.11, bf16[8,32,128]{2,1,0:T(8,128)(2,1)} %copy-done.12, ...), custom_call_target="tpu_custom_call" | custom-call | tf_op jit(solution)/shard_map/values/pallas_call | solution.py:417
  112.7 3.2 %collective-permute-start.9 = (bf16[8,256,128]{2,1,0:T(8,128)(2,1)}, bf16[8,256,128]{2,1,0:T(8,128)(2,1)S(1)}, u32[]{:S(2)}, u32[]{:S(2)}) collective-permute-start(bf16[8,256,128]{2,1,0:T(8,128)(2,1)} %values.1.v0), channel_id=1, source_target_pairs={{0,8},{8,16},{16,24},{24,0},{32,40},{40,48},{48,56},{56,32},{64,72... | collective-permute-start | bytes 1572872 | tf_op jit(solution)/shard_map/ppermute | solution.py:315
  115.9 0.0 collective-permute-start.11
  115.9 0.0 collective-permute-done.1.k1
  116.0 3.7 %collective-permute-start.2 = (bf16[4,256,128]{2,1,0:T(8,128)(2,1)S(1)}, bf16[4,256,128]{2,1,0:T(8,128)(2,1)S(1)}, u32[]{:S(2)}, u32[]{:S(2)}) collective-permute-start(bf16[4,256,128]{2,1,0:T(8,128)(2,1)S(1)} %slice.30), channel_id=1, source_target_pairs={{0,8},{8,16},{16,24},{24,0},{32,40},{40,48},{48,56},{56,32},{64,72... | collective-permute-start | bytes 786440 | tf_op jit(solution)/shard_map/ppermute | solution.py:319
  119.7 0.0 collective-permute-done.3.k4
  119.7 0.1 collective-permute-start.4
  119.8 8.8 %collective-permute-done.9.v1 = bf16[8,256,128]{2,1,0:T(8,128)(2,1)S(1)} collective-permute-done((bf16[8,256,128]{2,1,0:T(8,128)(2,1)}, bf16[8,256,128]{2,1,0:T(8,128)(2,1)S(1)}, u32[]{:S(2)}, u32[]{:S(2)}) %collective-permute-start.9) | collective-permute-done | bytes 524320 | tf_op jit(solution)/shard_map/ppermute | solution.py:315
  128.6 3.7 %collective-permute-start.10 = (bf16[4,256,128]{2,1,0:T(8,128)(2,1)S(1)}, bf16[4,256,128]{2,1,0:T(8,128)(2,1)S(1)}, u32[]{:S(2)}, u32[]{:S(2)}) collective-permute-start(bf16[4,256,128]{2,1,0:T(8,128)(2,1)S(1)} %slice.33), channel_id=1, source_target_pairs={{0,8},{8,16},{16,24},{24,0},{32,40},{40,48},{48,56},{56,32},{64,72... | collective-permute-start | bytes 786440 | tf_op jit(solution)/shard_map/ppermute | solution.py:319
  132.3 0.0 collective-permute-done.11.v4
  132.3 0.3 collective-permute-start.12
  132.6 1.5 collective-permute-done.2.k2
  134.0 3.4 %collective-permute-done.4.k3 = bf16[4,256,128]{2,1,0:T(8,128)(2,1)S(1)} collective-permute-done((bf16[4,256,128]{2,1,0:T(8,128)(2,1)S(1)}, bf16[4,256,128]{2,1,0:T(8,128)(2,1)S(1)}, u32[]{:S(2)}, u32[]{:S(2)}) %collective-permute-start.4) | collective-permute-done | bytes 262176 | tf_op jit(solution)/shard_map/ppermute | solution.py:320
  137.4 5.7 %peaks.1.peak_ref = f32[2048,128]{1,0:T(8,128)S(1)} custom-call(s32[2]{0:T(128)S(1)} %copy-done.7, bf16[8,256,128]{2,1,0:T(8,128)(2,1)S(1)} %get-tuple-element.24.q_ref, bf16[8,256,128]{2,1,0:T(8,128)(2,1)S(1)} %get-tuple-element.23.k0, bf16[8,256,128]{2,1,0:T(8,128)(2,1)S(1)} %collective-permute-done.1.k1, ...), custom_call_target="tpu_custom_call" | custom-call | tf_op jit(solution)/shard_map/peaks/pallas_call | solution.py:443
  143.1 8.5 %near.1 = (f32[2048,128]{1,0:T(8,128)S(1)}, f32[2048,128]{1,0:T(8,128)S(1)}) custom-call(s32[2]{0:T(128)S(1)} %copy-done.7, bf16[8,256,128]{2,1,0:T(8,128)(2,1)S(1)} %get-tuple-element.24.q_ref, f32[2048,128]{1,0:T(8,128)S(1)} %peaks.1.peak_ref, bf16[8,256,128]{2,1,0:T(8,128)(2,1)S(1)} %get-tuple-element.23.k0, ...), custom_call_target="tpu_custom_call" | custom-call | tf_op jit(solution)/shard_map/near/pallas_call | solution.py:455
  151.6 0.0 collective-permute-done.10.v2
  151.7 0.0 collective-permute-done.12.v3
  151.7 3.3 %far.1 = bf16[8,256,128]{2,1,0:T(8,128)(2,1)S(1)} custom-call(s32[2]{0:T(128)S(1)} %copy-done.7, bf16[8,256,128]{2,1,0:T(8,128)(2,1)S(1)} %get-tuple-element.24.q_ref, f32[2048,128]{1,0:T(8,128)S(1)} %peaks.1.peak_ref, bf16[4,256,128]{2,1,0:T(8,128)(2,1)S(1)} %collective-permute-done.2.k2, bf16[4,256,128]{2,1,0:T(8,128)(2,1)S(1)} %collective-permute-done.4.k3, ...), custom_call_target="tpu_custom_call" | custom-call | tf_op jit(solution)/shard_map/far/pallas_call | solution.py:463
  155.0 16.4 %all_to_all.16 = bf16[8,256,128]{2,1,0:T(8,128)(2,1)S(1)} all-to-all(bf16[8,256,128]{2,1,0:T(8,128)(2,1)S(1)} %far.1), channel_id=1, replica_groups={{0,32,64,96,128,160,192,224},{8,40,72,104,136,168,200,232},{16,48,80,11..., dimensions={0} | all-to-all | bytes 1048576 | tf_op jit(solution)/shard_map/all_to_all | solution.py:310
  171.3 0.2 copy.21
  171.6 1.0 copy.22
  (31 shorter events, 0.1 us)
Async XLA Ops:
  0.0 7.3 %copy-start.17 = (bf16[64,7]{0,1:T(8,128)(2,1)S(1)}, bf16[64,7]{0,1:T(8,128)(2,1)}, u32[]{:S(2)}) copy-start(bf16[64,7]{0,1:T(8,128)(2,1)} %param.18) | copy-start | bytes 2692
  3.6 5.8 %collective-permute-start = (bf16[8,1024]{1,0:T(8,128)(2,1)}, bf16[8,1024]{1,0:T(8,128)(2,1)S(1)}, u32[]{:S(2)}, u32[]{:S(2)}) collective-permute-start(bf16[8,1024]{1,0:T(8,128)(2,1)} %edge.1), channel_id=1, source_target_pairs={{0,8},{8,16},{16,24},{24,32},{32,40},{40,48},{48,56},{56,64},{64,7... | collective-permute-start | bytes 49160 | tf_op jit(solution)/shard_map/ppermute | solution.py:348
  7.5 13.4 %copy-start.14 = (f32[64,16]{0,1:T(8,128)S(1)}, f32[64,16]{0,1:T(8,128)}, u32[]{:S(2)}) copy-start(f32[64,16]{0,1:T(8,128)} %param.24) | copy-start | bytes 12292
  7.5 13.5 %copy-start.15 = (f32[64,16]{0,1:T(8,128)S(1)}, f32[64,16]{0,1:T(8,128)}, u32[]{:S(2)}) copy-start(f32[64,16]{0,1:T(8,128)} %param.25) | copy-start | bytes 12292
  9.4 0.6 copy-start.16
  15.1 12.6 %collective-permute-start.5 = (bf16[128,1024]{1,0:T(8,128)(2,1)}, bf16[128,1024]{1,0:T(8,128)(2,1)S(1)}, u32[]{:S(2)}, u32[]{:S(2)}) collective-permute-start(bf16[128,1024]{1,0:T(8,128)(2,1)} %get-tuple-element.19), channel_id=1, source_target_pairs={{0,8},{8,16},{16,24},{24,32},{32,40},{40,48},{48,56},{56,64},{64,7... | collective-permute-start | bytes 786440 | tf_op jit(solution)/shard_map/ppermute | solution.py:375
  21.1 2.7 %copy-start.6 = (bf16[64,128]{1,0:T(8,128)(2,1)S(1)}, bf16[64,128]{1,0:T(8,128)(2,1)}, u32[]{:S(2)}) copy-start(bf16[64,128]{1,0:T(8,128)(2,1)} %mr_ref.1) | copy-start | bytes 49156
  21.1 6.6 %copy-start.1 = (bf16[256,1024]{1,0:T(8,128)(2,1)S(1)}, bf16[256,1024]{1,0:T(8,128)(2,1)}, u32[]{:S(2)}) copy-start(bf16[256,1024]{1,0:T(8,128)(2,1)} %liq_ref.1) | copy-start | bytes 1572868
  21.1 6.6 %copy-start.2 = (bf16[256,1024]{1,0:T(8,128)(2,1)S(1)}, bf16[256,1024]{1,0:T(8,128)(2,1)}, u32[]{:S(2)}) copy-start(bf16[256,1024]{1,0:T(8,128)(2,1)} %mrq_ref.1) | copy-start | bytes 1572868
  21.1 6.6 %copy-start.3 = (bf16[256,1024]{1,0:T(8,128)(2,1)S(1)}, bf16[256,1024]{1,0:T(8,128)(2,1)}, u32[]{:S(2)}) copy-start(bf16[256,1024]{1,0:T(8,128)(2,1)} %lik_ref.1) | copy-start | bytes 1572868
  21.1 6.6 %copy-start.4 = (bf16[256,1024]{1,0:T(8,128)(2,1)S(1)}, bf16[256,1024]{1,0:T(8,128)(2,1)}, u32[]{:S(2)}) copy-start(bf16[256,1024]{1,0:T(8,128)(2,1)} %get-tuple-element.20.stream_ref) | copy-start | bytes 1572868
  21.1 6.6 %copy-start.5 = (bf16[256,1024]{1,0:T(8,128)(2,1)S(1)}, bf16[256,1024]{1,0:T(8,128)(2,1)}, u32[]{:S(2)}) copy-start(bf16[256,1024]{1,0:T(8,128)(2,1)} %get-tuple-element.18.in_ref) | copy-start | bytes 1572868
  61.2 5.8 %copy-start.9 = (bf16[8,288,128]{2,1,0:T(8,128)(2,1)}, bf16[8,288,128]{2,1,0:T(8,128)(2,1)S(1)}, u32[]{:S(2)}) copy-start(bf16[8,288,128]{2,1,0:T(8,128)(2,1)S(1)} %all_to_all.15.refs_1_) | copy-start | bytes 1769476
  61.2 40.3 %all-to-all-start = ((bf16[8,768,128]{2,1,0:T(8,128)(2,1)}), bf16[8,768,128]{2,1,0:T(8,128)(2,1)S(1)}, u32[]{:S(2)}, u32[]{:S(2)}) async-start(bf16[8,768,128]{2,1,0:T(8,128)(2,1)} %pack.1), calls=%async_computation | async-start | bytes 3145728 | tf_op jit(solution)/shard_map/all_to_all | solution.py:310
  67.0 39.0 %copy-start.10 = (bf16[8,32,128]{2,1,0:T(8,128)(2,1)}, bf16[8,32,128]{2,1,0:T(8,128)(2,1)S(1)}, u32[]{:S(2)}) copy-start(bf16[8,32,128]{2,1,0:T(8,128)(2,1)S(1)} %slice.32.refs_2_) | copy-start | bytes 196612
  67.0 38.9 %collective-permute-start.6 = (bf16[8,32,128]{2,1,0:T(8,128)(2,1)S(1)}, bf16[8,32,128]{2,1,0:T(8,128)(2,1)S(1)}, u32[]{:S(2)}, u32[]{:S(2)}) collective-permute-start(bf16[8,32,128]{2,1,0:T(8,128)(2,1)S(1)} %slice.32.refs_2_), channel_id=1, source_target_pairs={{0,8},{8,16},{16,24},{24,0},{32,40},{40,48},{48,56},{56,32},{64,72... | collective-permute-start | bytes 196616 | tf_op jit(solution)/shard_map/ppermute | solution.py:403
  70.1 35.8 %collective-permute-start.7 = (bf16[8,32,128]{2,1,0:T(8,128)(2,1)S(1)}, bf16[8,32,128]{2,1,0:T(8,128)(2,1)S(1)}, u32[]{:S(2)}, u32[]{:S(2)}) collective-permute-start(bf16[8,32,128]{2,1,0:T(8,128)(2,1)S(1)} %slice.32.refs_2_), channel_id=1, source_target_pairs={{0,16},{8,24},{16,0},{24,8},{32,48},{40,56},{48,32},{56,40},{64,80... | collective-permute-start | bytes 196616 | tf_op jit(solution)/shard_map/ppermute | solution.py:403
  70.1 35.8 %collective-permute-start.8 = (bf16[8,32,128]{2,1,0:T(8,128)(2,1)S(1)}, bf16[8,32,128]{2,1,0:T(8,128)(2,1)S(1)}, u32[]{:S(2)}, u32[]{:S(2)}) collective-permute-start(bf16[8,32,128]{2,1,0:T(8,128)(2,1)S(1)} %slice.32.refs_2_), channel_id=1, source_target_pairs={{0,24},{8,0},{16,8},{24,16},{32,56},{40,32},{48,40},{56,48},{64,88... | collective-permute-start | bytes 196616 | tf_op jit(solution)/shard_map/ppermute | solution.py:403
  101.5 1.2 copy-start.8
  102.7 13.3 %collective-permute-start.1 = (bf16[8,256,128]{2,1,0:T(8,128)(2,1)S(1)}, bf16[8,256,128]{2,1,0:T(8,128)(2,1)S(1)}, u32[]{:S(2)}, u32[]{:S(2)}) collective-permute-start(bf16[8,256,128]{2,1,0:T(8,128)(2,1)S(1)} %get-tuple-element.23.k0), channel_id=1, source_target_pairs={{0,8},{8,16},{16,24},{24,0},{32,40},{40,48},{48,56},{56,32},{64,72... | collective-permute-start | bytes 1572872 | tf_op jit(solution)/shard_map/ppermute | solution.py:315
  105.9 13.8 %collective-permute-start.3 = (bf16[8,256,128]{2,1,0:T(8,128)(2,1)S(1)}, bf16[8,256,128]{2,1,0:T(8,128)(2,1)S(1)}, u32[]{:S(2)}, u32[]{:S(2)}) collective-permute-start(bf16[8,256,128]{2,1,0:T(8,128)(2,1)S(1)} %get-tuple-element.23.k0), channel_id=1, source_target_pairs={{0,24},{8,0},{16,8},{24,16},{32,56},{40,32},{48,40},{56,48},{64,88... | collective-permute-start | bytes 1572872 | tf_op jit(solution)/shard_map/ppermute | solution.py:316
  105.9 0.6 copy-start.11
  105.9 0.6 copy-start.12
  106.0 0.6 copy-start.13
  112.7 24.7 %copy-start.7 = (s32[2]{0:T(128)S(1)}, s32[2]{0:T(128)}, u32[]{:S(2)}) copy-start(s32[2]{0:T(128)} %pad_add_fusion.where_ref.refs_0_) | copy-start | bytes 28
  112.7 15.9 %collective-permute-start.9 = (bf16[8,256,128]{2,1,0:T(8,128)(2,1)}, bf16[8,256,128]{2,1,0:T(8,128)(2,1)S(1)}, u32[]{:S(2)}, u32[]{:S(2)}) collective-permute-start(bf16[8,256,128]{2,1,0:T(8,128)(2,1)} %values.1.v0), channel_id=1, source_target_pairs={{0,8},{8,16},{16,24},{24,0},{32,40},{40,48},{48,56},{56,32},{64,72... | collective-permute-start | bytes 1572872 | tf_op jit(solution)/shard_map/ppermute | solution.py:315
  115.9 16.3 %collective-permute-start.11 = (bf16[8,256,128]{2,1,0:T(8,128)(2,1)}, bf16[8,256,128]{2,1,0:T(8,128)(2,1)S(1)}, u32[]{:S(2)}, u32[]{:S(2)}) collective-permute-start(bf16[8,256,128]{2,1,0:T(8,128)(2,1)} %values.1.v0), channel_id=1, source_target_pairs={{0,24},{8,0},{16,8},{24,16},{32,56},{40,32},{48,40},{56,48},{64,88... | collective-permute-start | bytes 1572872 | tf_op jit(solution)/shard_map/ppermute | solution.py:316
  116.0 18.0 %collective-permute-start.2 = (bf16[4,256,128]{2,1,0:T(8,128)(2,1)S(1)}, bf16[4,256,128]{2,1,0:T(8,128)(2,1)S(1)}, u32[]{:S(2)}, u32[]{:S(2)}) collective-permute-start(bf16[4,256,128]{2,1,0:T(8,128)(2,1)S(1)} %slice.30), channel_id=1, source_target_pairs={{0,8},{8,16},{16,24},{24,0},{32,40},{40,48},{48,56},{56,32},{64,72... | collective-permute-start | bytes 786440 | tf_op jit(solution)/shard_map/ppermute | solution.py:319
  119.7 17.7 %collective-permute-start.4 = (bf16[4,256,128]{2,1,0:T(8,128)(2,1)S(1)}, bf16[4,256,128]{2,1,0:T(8,128)(2,1)S(1)}, u32[]{:S(2)}, u32[]{:S(2)}) collective-permute-start(bf16[4,256,128]{2,1,0:T(8,128)(2,1)S(1)} %slice.31), channel_id=1, source_target_pairs={{0,24},{8,0},{16,8},{24,16},{32,56},{40,32},{48,40},{56,48},{64,88... | collective-permute-start | bytes 786440 | tf_op jit(solution)/shard_map/ppermute | solution.py:320
  128.6 23.1 %collective-permute-start.10 = (bf16[4,256,128]{2,1,0:T(8,128)(2,1)S(1)}, bf16[4,256,128]{2,1,0:T(8,128)(2,1)S(1)}, u32[]{:S(2)}, u32[]{:S(2)}) collective-permute-start(bf16[4,256,128]{2,1,0:T(8,128)(2,1)S(1)} %slice.33), channel_id=1, source_target_pairs={{0,8},{8,16},{16,24},{24,0},{32,40},{40,48},{48,56},{56,32},{64,72... | collective-permute-start | bytes 786440 | tf_op jit(solution)/shard_map/ppermute | solution.py:319
  132.3 19.4 %collective-permute-start.12 = (bf16[4,256,128]{2,1,0:T(8,128)(2,1)S(1)}, bf16[4,256,128]{2,1,0:T(8,128)(2,1)S(1)}, u32[]{:S(2)}, u32[]{:S(2)}) collective-permute-start(bf16[4,256,128]{2,1,0:T(8,128)(2,1)S(1)} %slice.34), channel_id=1, source_target_pairs={{0,24},{8,0},{16,8},{24,16},{32,56},{40,32},{48,40},{56,48},{64,88... | collective-permute-start | bytes 786440 | tf_op jit(solution)/shard_map/ppermute | solution.py:320
  137.4 5.7 %copy-start = (bf16[8,256,128]{2,1,0:T(8,128)(2,1)S(1)}, bf16[8,256,128]{2,1,0:T(8,128)(2,1)}, u32[]{:S(2)}) copy-start(bf16[8,256,128]{2,1,0:T(8,128)(2,1)} %values.1.v0) | copy-start | bytes 1572868

commit v2 on v1

--- a/solution.py
+++ b/solution.py
@@ -113,8 +113,9 @@
     return total
 
 
-def conv_kernel(mr_tab, li_tab, in_ref, halo_ref, stream_ref, mrq_ref, lik_ref, liq_ref, out_ref):
-    at = pl.program_id(0)
+def conv_kernel(where_ref, mr_tab, li_tab, in_ref, halo_ref, stream_ref, mrq_ref, lik_ref, liq_ref, *outs):
+    step = pl.program_id(0)
+    at = lax.rem(where_ref[0] + step, len(outs))
     taps = halo_ref.shape[0]
     groups = mr_tab.shape[1] // taps
     modes = li_tab.shape[1] // groups - taps
@@ -134,14 +135,20 @@
     both = fold_groups(res, taps, groups, width)
     conv = jnp.concatenate([both[:, :LANES], both[:, LANES:]], 0)
     rows = conv.shape[0]
-    out_ref[0, 0:rows, :] = (stream_f + liq_ref[...].astype(F32) * conv).astype(BF16)
+    wide = (stream_f + liq_ref[...].astype(F32) * conv).astype(BF16)
     ends = res[groups * taps :, LANES:].reshape(modes, groups, LANES)
     mine = lax.broadcasted_iota(jnp.int32, (modes, groups, LANES), 2) // width
     mine = mine == lax.broadcasted_iota(jnp.int32, (modes, groups, LANES), 1)
     state = jnp.sum(jnp.where(mine, ends, 0.0), axis=1)
     high = state.astype(BF16)
-    out_ref[0, rows : rows + modes, :] = high
-    out_ref[0, rows + modes : rows + 2 * modes, :] = (state - high.astype(F32)).astype(BF16)
+    low = (state - high.astype(F32)).astype(BF16)
+    for s, out_ref in enumerate(outs):
+
+        @pl.when(step == s)
+        def _():
+            out_ref[0:rows, :] = wide
+            out_ref[rows : rows + modes, :] = high
+            out_ref[rows + modes : rows + 2 * modes, :] = low
 
 
 def pack_kernel(a_ref, b_ref, c_ref, out_ref):
@@ -151,42 +158,70 @@
             out_ref[j, n * rows : (n + 1) * rows, :] = ref[:, j * HEAD : (j + 1) * HEAD]
 
 
+def unpack(where, parts, cuts):
+    count = len(parts)
+    bounds = list(zip((0,) + cuts[:-1], cuts))
+    parts = [part.reshape(cuts[-1], LANES) for part in parts]
+
+    def body(where_ref, *refs):
+        for s in range(count):
+            z = lax.rem(where_ref[0] + count - s, count)
+            for (low, high), out_ref in zip(bounds, refs[count:]):
+                out_ref[z] = refs[s][low:high, :]
+
+    inside = pl.BlockSpec(memory_space=pltpu.VMEM)
+    return pl.pallas_call(
+        body,
+        in_specs=[pl.BlockSpec(memory_space=pltpu.SMEM)] + [inside] * count,
+        out_specs=[inside] * len(cuts),
+        out_shape=[jax.ShapeDtypeStruct((count, high - low, LANES), BF16) for low, high in bounds],
+        compiler_params=pltpu.CompilerParams(vmem_limit_bytes=16 * MIB),
+    )(where, *parts)
+
+
 def value_kernel(where_ref, pack_ref, all_ref, liq_ref, s1_ref, s2_ref, s3_ref, rate_ref, res_ref,
-                 total_len, out_ref, emit, carry):
-    i = pl.program_id(0)
-    blocks = all_ref.shape[0]
-    rows = out_ref.shape[1]
+                 total_len, out_ref, emit):
+    blocks, rows, _ = out_ref.shape
     modes = rate_ref.shape[0]
-
-    @pl.when(i == 0)
-    def _():
-        x = where_ref[1]
-        rate = rate_ref[...]
-        gain = res_ref[...] * jnp.sqrt(1.0 - jnp.exp(-2.0 * rate) + 1.0 / total_len)
-        step = (lax.broadcasted_iota(jnp.int32, (rows, LANES), 0) + 1).astype(F32)
+    x = where_ref[1]
+    rate = rate_ref[...]
+    step = (lax.broadcasted_iota(jnp.int32, (rows, LANES), 0) + 1).astype(F32)
+
+    @pl.loop(0, modes)
+    def _(m):
+        slow, strength = rate_ref[pl.ds(m, 1), :], res_ref[pl.ds(m, 1), :]
+        strength = strength * jnp.sqrt(1.0 - jnp.exp(-2.0 * slow) + 1.0 / total_len)
+        emit[m] = strength * jnp.exp(-slow * step)
+
+    decays = [jnp.exp(-rate * (rows * k)) for k in range(STRIPE + 1)]
+    scans = []
+    for part in (all_ref, s1_ref, s2_ref, s3_ref):
+        running = jnp.zeros((modes, LANES), F32)
+        seen = [running]
+        for b in range(blocks):
+            here = part[b, 0:modes, :].astype(F32) + part[b, modes : 2 * modes, :].astype(F32)
+            running = running * decays[STRIPE] + here
+            seen.append(running)
+        scans.append(seen)
+    carries = []
+    for b in range(blocks):
+        total = decays[STRIPE - 1] * scans[0][b]
+        for k in range(1, STRIPE):
+            total = total + decays[k - 1] * jnp.where(x >= k, scans[k][b + 1], scans[k][b])
+        carries.append(total)
+    piece = 32
+
+    @pl.loop(0, rows // piece)
+    def _(r):
+        place = pl.ds(pl.multiple_of(r * piece, piece), piece)
+        convs = [jnp.zeros((piece, LANES), F32)] * blocks
         for m in range(modes):
-            emit[m] = gain[m : m + 1, :] * jnp.exp(-rate[m : m + 1, :] * step)
-        decays = [jnp.exp(-rate * (rows * k)) for k in range(STRIPE + 1)]
-        scans = []
-        for part in (all_ref, s1_ref, s2_ref, s3_ref):
-            running = jnp.zeros((modes, LANES), F32)
-            seen = [running]
-            for b in range(blocks):
-                here = part[b, 0:modes, :].astype(F32) + part[b, modes : 2 * modes, :].astype(F32)
-                running = running * decays[STRIPE] + here
-                seen.append(running)
-            scans.append(seen)
-        for b in range(blocks):
-            total = decays[STRIPE - 1] * scans[0][b]
-            for k in range(1, STRIPE):
-                total = total + decays[k - 1] * jnp.where(x >= k, scans[k][b + 1], scans[k][b])
-            carry[b] = total
-
-    conv = jnp.zeros((rows, LANES), F32)
-    for m in range(modes):
-        conv = conv + emit[m] * carry[i, m : m + 1, :]
-    value = (pack_ref[0].astype(F32) + liq_ref[0].astype(F32) * conv).astype(BF16)
-    out_ref[0] = value
+            table = emit[m, place, :]
+            convs = [conv + table * carries[b][m : m + 1, :] for b, conv in enumerate(convs)]
+        for b, conv in enumerate(convs):
+            out_ref[b, place, :] = (
+                pack_ref[b, place, :].astype(F32) + liq_ref[b, place, :].astype(F32) * conv
+            ).astype(BF16)
 
 
 def causal(scores, x, k, rows):
@@ -311,6 +346,15 @@
             packed, "seq", split_axis=0, concat_axis=0, tiled=True, axis_index_groups=columns
         )
 
+    def shifted(parts):
+        return [parts[0]] + [
+            lax.ppermute(
+                part, "seq", [(d, (d // STRIPE + s) % depth * STRIPE + d % STRIPE) for d in range(seq)]
+            )
+            for s, part in enumerate(parts)
+            if s
+        ]
+
     def spread(part):
         behind = lax.ppermute(part, "seq", turn(1))
         ahead = lax.ppermute(part, "seq", turn(STRIPE - 1))
@@ -321,6 +365,8 @@
         ]
         return part, behind, *across, ahead
 
+    inside = pl.BlockSpec(memory_space=pltpu.VMEM)
+    small = pltpu.CompilerParams(vmem_limit_bytes=16 * MIB)
     early = pl.pallas_call(
         pack_kernel,
         grid=(2,),
@@ -373,72 +419,50 @@
         name="short",
     )(tok, embed_table, edge, se_query, se_key, se_weights, mr_key)
     mr_edge = lax.ppermute(mr_tail, "seq", forward)
-    early, mr_input = lax.optimization_barrier((early, mr_input))
     early = exchange(early)
 
-    column = pl.BlockSpec((rows, LANES), lambda j: (0, j))
+    column = pl.BlockSpec((rows, LANES), lambda j, w: (0, lax.rem(w[0] + j, heads)))
+    ends = pl.BlockSpec((taps, LANES), lambda j, w: (0, lax.rem(w[0] + j, heads)))
+    size = (rows + 2 * modes, LANES)
     packed = pl.pallas_call(
         conv_kernel,
-        grid=(heads,),
-        in_specs=[
-            pl.BlockSpec(memory_space=pltpu.VMEM),
-            pl.BlockSpec(memory_space=pltpu.VMEM),
-            column,
-            pl.BlockSpec((taps, LANES), lambda j: (0, j)),
-            column,
-            column,
-            column,
-            column,
-        ],
-        out_specs=pl.BlockSpec((1, rows + 2 * modes, LANES), lambda j: (j, 0, 0)),
-        out_shape=jax.ShapeDtypeStruct((heads, rows + 2 * modes, LANES), BF16),
+        grid_spec=pltpu.PrefetchScalarGridSpec(
+            num_scalar_prefetch=1,
+            grid=(heads,),
+            in_specs=[inside, inside, column, ends, column, column, column, column],
+            out_specs=[pl.BlockSpec(size, lambda j, w: (0, 0))] * heads,
+        ),
+        out_shape=[jax.ShapeDtypeStruct(size, BF16)] * heads,
         compiler_params=pltpu.CompilerParams(vmem_limit_bytes=24 * MIB),
         name="medium_long",
-    )(mr_tab, li_tab, mr_input, mr_edge, stream, mr_query, li_key, li_query)
-    packed = exchange(packed)
-
-    query = early[:, :rows]
-    keys = spread(early[:, rows : 2 * rows])
-    states = packed[:, rows:]
+    )(where, mr_tab, li_tab, mr_input, mr_edge, stream, mr_query, li_key, li_query)
+    packed = shifted(packed)
+
+    query, key, early_gate = (early[:, n * rows : (n + 1) * rows] for n in range(3))
+    keys = spread(key)
+    packed, states = unpack(where, packed, (rows, rows + 2 * modes))
     others = [lax.ppermute(states, "seq", turn(k)) for k in range(1, STRIPE)]
 
-    def per_channel(value):
-        value = jnp.broadcast_to(value.T[:, :, None], (modes, group_count, width))
-        return value.reshape(modes, channels)
-
     def mine(value):
-        return lax.dynamic_slice_in_dim(per_channel(value), where[0] * HEAD, HEAD, axis=1)
+        count = HEAD // width
+        value = lax.dynamic_slice_in_dim(value, where[0] * count, count, axis=0)
+        value = jnp.broadcast_to(value.T[:, :, None], (modes, count, width))
+        return value.reshape(modes, HEAD)
 
     def value_body(*refs):
         value_kernel(*refs[:9], total_len, *refs[9:])
 
-    state_spec = whole((depth, 2 * modes, LANES))
-    block = pl.BlockSpec((1, rows, LANES), lambda i: (i, 0, 0))
     values = pl.pallas_call(
         value_body,
-        grid=(depth,),
-        in_specs=[
-            smem,
-            block,
-            state_spec,
-            pl.BlockSpec((1, rows, LANES), lambda i: (i, 2, 0)),
-            state_spec,
-            state_spec,
-            state_spec,
-            whole((modes, LANES)),
-            whole((modes, LANES)),
-        ],
-        out_specs=block,
+        in_specs=[smem] + [inside] * 8,
+        out_specs=inside,
         out_shape=jax.ShapeDtypeStruct((depth, rows, LANES), BF16),
-        scratch_shapes=[
-            pltpu.VMEM((modes, rows, LANES), F32),
-            pltpu.VMEM((depth, modes, LANES), F32),
-        ],
+        scratch_shapes=[pltpu.VMEM((modes, rows, LANES), F32)],
+        compiler_params=small,
         name="values",
-    )(where, packed, states, early, *others, mine(li_rate), mine(li_residue))
+    )(where, packed, states, early_gate, *others, mine(li_rate), mine(li_residue))
     values = spread(values)
 
-    inside = pl.BlockSpec(memory_space=pltpu.VMEM)
     reach = depth * rows
     peaks = pl.pallas_call(
         peak_kernel,

time: 173 us -> 176 us (1.017)
  the two profiles are of different devices: /device:TPU:22 before, /device:TPU:6 now
where the time goes in v2:
time: 176 us; the launch traced here: 175 us
  starting transfers between devices  57.4 us (33%)
  waiting for transfers between devices  47.7 us (27%)
  Pallas kernels  43.5 us (25%)
  blocking collectives  18.6 us (11%)
  local copies, waits for them, and re-layouts  7.72 us (4%)
    ppermute x1, waiting for transfers between devices, local(): edge = lax.ppermute(edge, 'seq', forward)  24.4 us
    ppermute x7, starting transfers between devices, shifted(): lax.ppermute(part, 'seq', [(d, (d // STRIPE + s) % depth * STRIPE + d % S...  19.3 us
    all_to_all x1, blocking collectives, exchange(): lax.all_to_all(packed, 'seq', split_axis=0, concat_axis=0, tiled=True, ax...  18.6 us
    ppermute x2, waiting for transfers between devices, spread(): behind = lax.ppermute(part, 'seq', turn(1))  13.4 us
    pallas_call x1, Pallas kernels, local(): pl.pallas_call(conv_kernel, grid_spec=pltpu.PrefetchScalarGridSpec(num_sc...  9.47 us
    all_to_all x1, starting transfers between devices, exchange(): lax.all_to_all(packed, 'seq', split_axis=0, concat_axis=0, tiled=True, ax...  8.6 us
    pallas_call x1, Pallas kernels, local(): pl.pallas_call(near_kernel, in_specs=[smem] + [inside] * 8, out_specs=[in...  8.45 us
    ppermute x3, starting transfers between devices, local(): others = [lax.ppermute(states, 'seq', turn(k)) for k in range(1, STRIPE)]  7.27 us
  transfers between devices with their start and end apart: 21, of which 10 were waited for; matrix products, arithmetic and copies ran while one was open for 2% of the time, Pallas kernels for 22%

profile of v2, /device:TPU:6, one launch (start us, length us, event | category | flops | bytes accessed | tf_op | source)
XLA Modules:
  0.0 175.3 jit_solution(7265566308649002872)
XLA Ops:
  0.0 2.4 %pack.1 = bf16[8,768,128]{2,1,0:T(8,128)(2,1)} custom-call(bf16[256,1024]{1,0:T(8,128)(2,1)} %a_ref.1, bf16[256,1024]{1,0:T(8,128)(2,1)} %b_ref.1, bf16[256,1024]{1,0:T(8,128)(2,1)} %liq_ref.1), custom_call_target="tpu_custom_call" | custom-call | tf_op jit(solution)/shard_map/pack/pallas_call | solution.py:370
  2.4 8.6 %all-to-all-start = ((bf16[8,768,128]{2,1,0:T(8,128)(2,1)}), bf16[8,768,128]{2,1,0:T(8,128)(2,1)}, u32[]{:S(2)}, u32[]{:S(2)}) async-start(bf16[8,768,128]{2,1,0:T(8,128)(2,1)} %pack.1), calls=%async_computation | async-start | bytes 3145728 | tf_op jit(solution)/shard_map/all_to_all | solution.py:345
  11.0 0.8 copy.20.tok_ref
  11.8 2.1 %edge.1 = bf16[8,1024]{1,0:T(8,128)(2,1)} custom-call(s32[256,1]{1,0:T(8,128)} %copy.20.tok_ref, bf16[512,1024]{1,0:T(8,128)(2,1)} %table_ref.3, bf16[256,1024]{1,0:T(8,128)(2,1)} %key_ref.3), custom_call_target="tpu_custom_call" | custom-call | tf_op jit(solution)/shard_map/edge/pallas_call | solution.py:382
  13.9 3.8 %collective-permute-start.4 = (bf16[8,1024]{1,0:T(8,128)(2,1)}, bf16[8,1024]{1,0:T(8,128)(2,1)S(1)}, u32[]{:S(2)}, u32[]{:S(2)}) collective-permute-start(bf16[8,1024]{1,0:T(8,128)(2,1)} %edge.1), channel_id=1, source_target_pairs={{0,8},{8,16},{16,24},{24,32},{32,40},{40,48},{48,56},{56,64},{64,7... | collective-permute-start | bytes 49160 | tf_op jit(solution)/shard_map/ppermute | solution.py:394
  17.8 0.1 broadcast_in_dim.9
  17.9 0.0 copy-start.6
  17.9 0.0 copy-start.7
  17.9 0.0 copy-start.5
  17.9 0.7 reshape.15.filt_ref
  18.7 24.4 %collective-permute-done.4.edge_ref = bf16[8,1024]{1,0:T(8,128)(2,1)S(1)} collective-permute-done((bf16[8,1024]{1,0:T(8,128)(2,1)}, bf16[8,1024]{1,0:T(8,128)(2,1)S(1)}, u32[]{:S(2)}, u32[]{:S(2)}) %collective-permute-start.4) | collective-permute-done | bytes 16416 | tf_op jit(solution)/shard_map/ppermute | solution.py:394
  43.1 0.6 copy-done.8
  43.7 5.0 %short.1 = (bf16[256,1024]{1,0:T(8,128)(2,1)}, bf16[256,1024]{1,0:T(8,128)(2,1)}, bf16[128,1024]{1,0:T(8,128)(2,1)}) custom-call(s32[256,1]{1,0:T(8,128)} %copy.20.tok_ref, bf16[512,1024]{1,0:T(8,128)(2,1)} %table_ref.3, bf16[8,1024]{1,0:T(8,128)(2,1)} %copy-done.8, bf16[256,1024]{1,0:T(8,128)(2,1)} %query_ref.1, bf16[256,1024]{1,0:T(8,128)(2,1)} %key_ref.3, ...), custom_call_target="tpu_custom_call" | custom-call | tf_op jit(solution)/shard_map/short/pallas_call | solution.py:404
  48.7 6.5 %collective-permute-start.5 = (bf16[128,1024]{1,0:T(8,128)(2,1)}, bf16[128,1024]{1,0:T(8,128)(2,1)S(1)}, u32[]{:S(2)}, u32[]{:S(2)}) collective-permute-start(bf16[128,1024]{1,0:T(8,128)(2,1)} %get-tuple-element.25), channel_id=1, source_target_pairs={{0,8},{8,16},{16,24},{24,32},{32,40},{40,48},{48,56},{56,64},{64,7... | collective-permute-start | bytes 786440 | tf_op jit(solution)/shard_map/ppermute | solution.py:421
  55.2 0.1 copy.17.rate_ref
  55.3 0.1 copy.18.res_ref
  55.4 3.9 %tables.1 = (bf16[8,1024,256]{2,1,0:T(8,128)(2,1)S(1)}, bf16[8,1152,256]{2,1,0:T(8,128)(2,1)S(1)}) custom-call(bf16[64,128]{1,0:T(8,128)(2,1)S(1)} %copy-done.5, f32[64,16]{1,0:T(8,128)S(1)} %copy.17.rate_ref, f32[64,16]{1,0:T(8,128)S(1)} %copy.18.res_ref), custom_call_target="tpu_custom_call" | custom-call | tf_op jit(solution)/shard_map/tables/pallas_call | solution.py:62
  59.3 0.1 pad_add_fusion.where_ref.refs_0_
  59.4 0.4 collective-permute-done.5.halo_ref
  59.8 1.0 copy-done.3
  60.9 1.0 copy-done.4
  61.9 9.5 %medium_long.1 = (bf16[288,128]{1,0:T(8,128)(2,1)S(1)}, bf16[288,128]{1,0:T(8,128)(2,1)S(1)}, bf16[288,128]{1,0:T(8,128)(2,1)S(1)}, bf16[288,128]{1,0:T(8,128)(2...) custom-call(s32[2]{0:T(128)S(1)} %pad_add_fusion.where_ref.refs_0_, ...), custom_call_target="tpu_custom_call" | custom-call | tf_op jit(solution)/shard_map/medium_long/pallas_call | solution.py:427
  71.4 0.1 collective-permute-start.10
  71.5 9.1 %collective-permute-start.11 = (bf16[288,128]{1,0:T(8,128)(2,1)S(1)}, bf16[288,128]{1,0:T(8,128)(2,1)S(1)}, u32[]{:S(2)}, u32[]{:S(2)}) collective-permute-start(bf16[288,128]{1,0:T(8,128)(2,1)S(1)} %get-tuple-element.33), channel_id=1, source_target_pairs={{0,192},{8,200},{16,208},{24,216},{32,224},{40,232},{48,240},{56,2... | collective-permute-start | bytes 221192 | tf_op jit(solution)/shard_map/ppermute | solution.py:351
  80.6 0.9 collective-permute-start.12
  81.6 1.1 collective-permute-start.6
  82.7 1.5 collective-permute-start.7
  84.1 0.0 collective-permute-done.10.refs_5_
  84.2 3.8 %collective-permute-start.8 = (bf16[288,128]{1,0:T(8,128)(2,1)S(1)}, bf16[288,128]{1,0:T(8,128)(2,1)S(1)}, u32[]{:S(2)}, u32[]{:S(2)}) collective-permute-start(bf16[288,128]{1,0:T(8,128)(2,1)S(1)} %get-tuple-element.30), channel_id=1, source_target_pairs={{0,96},{8,104},{16,112},{24,120},{32,128},{40,136},{48,144},{56,15... | collective-permute-start | bytes 221192 | tf_op jit(solution)/shard_map/ppermute | solution.py:351
  88.0 2.7 %collective-permute-start.9 = (bf16[288,128]{1,0:T(8,128)(2,1)S(1)}, bf16[288,128]{1,0:T(8,128)(2,1)S(1)}, u32[]{:S(2)}, u32[]{:S(2)}) collective-permute-start(bf16[288,128]{1,0:T(8,128)(2,1)S(1)} %get-tuple-element.31), channel_id=1, source_target_pairs={{0,128},{8,136},{16,144},{24,152},{32,160},{40,168},{48,176},{56,1... | collective-permute-start | bytes 221192 | tf_op jit(solution)/shard_map/ppermute | solution.py:351
  90.6 0.1 dynamic-slice_bitcast_fusion
  90.7 0.1 broadcast_in_dim.10
  90.8 0.1 reshape.16.refs_7_
  90.9 0.1 broadcast_in_dim.11
  91.0 0.1 reshape.17.refs_8_
  91.1 0.0 collective-permute-done.12.refs_7_
  91.1 2.6 %collective-permute-done.7.refs_2_ = bf16[288,128]{1,0:T(8,128)(2,1)S(1)} collective-permute-done((bf16[288,128]{1,0:T(8,128)(2,1)S(1)}, bf16[288,128]{1,0:T(8,128)(2,1)S(1)}, u32[]{:S(2)}, u32[]{:S(2)}) %collective-permute-start.7) | collective-permute-done | bytes 73760 | tf_op jit(solution)/shard_map/ppermute | solution.py:351
  93.7 0.9 collective-permute-done.8.refs_3_
  94.6 2.1 %collective-permute-done.9.refs_4_ = bf16[288,128]{1,0:T(8,128)(2,1)S(1)} collective-permute-done((bf16[288,128]{1,0:T(8,128)(2,1)S(1)}, bf16[288,128]{1,0:T(8,128)(2,1)S(1)}, u32[]{:S(2)}, u32[]{:S(2)}) %collective-permute-start.9) | collective-permute-done | bytes 73760 | tf_op jit(solution)/shard_map/ppermute | solution.py:351
  96.7 0.6 shard_map.136
  97.3 6.3 %collective-permute-start.13 = (bf16[8,32,128]{2,1,0:T(8,128)(2,1)S(1)}, bf16[8,32,128]{2,1,0:T(8,128)(2,1)S(1)}, u32[]{:S(2)}, u32[]{:S(2)}) collective-permute-start(bf16[8,32,128]{2,1,0:T(8,128)(2,1)S(1)} %get-tuple-element.36.refs_2_), channel_id=1, source_target_pairs={{0,8},{8,16},{16,24},{24,0},{32,40},{40,48},{48,56},{56,32},{64,72... | collective-permute-start | bytes 196616 | tf_op jit(solution)/shard_map/ppermute | solution.py:444
  103.6 0.0 collective-permute-start.14
  103.6 1.0 collective-permute-start.15
  104.5 1.5 fusion
  106.0 2.4 %collective-permute-start = (bf16[8,256,128]{2,1,0:T(8,128)(2,1)S(1)}, bf16[8,256,128]{2,1,0:T(8,128)(2,1)S(1)}, u32[]{:S(2)}, u32[]{:S(2)}) collective-permute-start(bf16[8,256,128]{2,1,0:T(8,128)(2,1)S(1)} %get-tuple-element.40.k0), channel_id=1, source_target_pairs={{0,8},{8,16},{16,24},{24,0},{32,40},{40,48},{48,56},{56,32},{64,72... | collective-permute-start | bytes 1572872 | tf_op jit(solution)/shard_map/ppermute | solution.py:359
  108.4 0.5 collective-permute-start.2
  108.9 1.1 collective-permute-done.14.refs_5_
  110.0 0.4 collective-permute-done.15.refs_6_
  110.5 2.6 %values.1.v0 = bf16[8,256,128]{2,1,0:T(8,128)(2,1)S(1)} custom-call(s32[2]{0:T(128)S(1)} %pad_add_fusion.where_ref.refs_0_, bf16[8,256,128]{2,1,0:T(8,128)(2,1)S(1)} %get-tuple-element.35.refs_1_, bf16[8,32,128]{2,1,0:T(8,128)(2,1)S(1)} %get-tuple-element.36.refs_2_, bf16[8,256,128]{2,1,0:T(8,128)(2,1)S(1)} %get-tuple-element.39.refs_3_, ...), custom_call_target="tpu_custom_call" | custom-call | tf_op jit(solution)/shard_map/values/pallas_call | solution.py:455
  113.1 1.6 collective-permute-start.16
  114.7 0.5 collective-permute-start.18
  115.2 6.3 %collective-permute-done.k1 = bf16[8,256,128]{2,1,0:T(8,128)(2,1)S(1)} collective-permute-done((bf16[8,256,128]{2,1,0:T(8,128)(2,1)S(1)}, bf16[8,256,128]{2,1,0:T(8,128)(2,1)S(1)}, u32[]{:S(2)}, u32[]{:S(2)}) %collective-permute-start) | collective-permute-done | bytes 524320 | tf_op jit(solution)/shard_map/ppermute | solution.py:359
  121.4 3.1 %collective-permute-start.1 = (bf16[4,256,128]{2,1,0:T(8,128)(2,1)S(1)}, bf16[4,256,128]{2,1,0:T(8,128)(2,1)S(1)}, u32[]{:S(2)}, u32[]{:S(2)}) collective-permute-start(bf16[4,256,128]{2,1,0:T(8,128)(2,1)S(1)} %slice.30), channel_id=1, source_target_pairs={{0,8},{8,16},{16,24},{24,0},{32,40},{40,48},{48,56},{56,32},{64,72... | collective-permute-start | bytes 786440 | tf_op jit(solution)/shard_map/ppermute | solution.py:363
  124.5 0.1 collective-permute-start.3
  124.6 7.2 %collective-permute-done.16.v1 = bf16[8,256,128]{2,1,0:T(8,128)(2,1)S(1)} collective-permute-done((bf16[8,256,128]{2,1,0:T(8,128)(2,1)S(1)}, bf16[8,256,128]{2,1,0:T(8,128)(2,1)S(1)}, u32[]{:S(2)}, u32[]{:S(2)}) %collective-permute-start.16) | collective-permute-done | bytes 524320 | tf_op jit(solution)/shard_map/ppermute | solution.py:359
  131.8 3.8 %collective-permute-start.17 = (bf16[4,256,128]{2,1,0:T(8,128)(2,1)S(1)}, bf16[4,256,128]{2,1,0:T(8,128)(2,1)S(1)}, u32[]{:S(2)}, u32[]{:S(2)}) collective-permute-start(bf16[4,256,128]{2,1,0:T(8,128)(2,1)S(1)} %slice.33), channel_id=1, source_target_pairs={{0,8},{8,16},{16,24},{24,0},{32,40},{40,48},{48,56},{56,32},{64,72... | collective-permute-start | bytes 786440 | tf_op jit(solution)/shard_map/ppermute | solution.py:363
  135.6 0.1 collective-permute-start.19
  135.7 2.3 %collective-permute-done.3.k3 = bf16[4,256,128]{2,1,0:T(8,128)(2,1)S(1)} collective-permute-done((bf16[4,256,128]{2,1,0:T(8,128)(2,1)S(1)}, bf16[4,256,128]{2,1,0:T(8,128)(2,1)S(1)}, u32[]{:S(2)}, u32[]{:S(2)}) %collective-permute-start.3) | collective-permute-done | bytes 262176 | tf_op jit(solution)/shard_map/ppermute | solution.py:364
  138.0 5.7 %peaks.1.peak_ref = f32[2048,128]{1,0:T(8,128)S(1)} custom-call(s32[2]{0:T(128)S(1)} %pad_add_fusion.where_ref.refs_0_, bf16[8,256,128]{2,1,0:T(8,128)(2,1)S(1)} %get-tuple-element.41.q_ref, bf16[8,256,128]{2,1,0:T(8,128)(2,1)S(1)} %get-tuple-element.40.k0, bf16[8,256,128]{2,1,0:T(8,128)(2,1)S(1)} %collective-permute-done.k1, ...), custom_call_target="tpu_custom_call" | custom-call | tf_op jit(solution)/shard_map/peaks/pallas_call | solution.py:467
  143.7 8.4 %near.1 = (f32[2048,128]{1,0:T(8,128)S(1)}, f32[2048,128]{1,0:T(8,128)S(1)}) custom-call(s32[2]{0:T(128)S(1)} %pad_add_fusion.where_ref.refs_0_, bf16[8,256,128]{2,1,0:T(8,128)(2,1)S(1)} %get-tuple-element.41.q_ref, f32[2048,128]{1,0:T(8,128)S(1)} %peaks.1.peak_ref, bf16[8,256,128]{2,1,0:T(8,128)(2,1)S(1)} %get-tuple-element.40.k0, ...), custom_call_target="tpu_custom_call" | custom-call | tf_op jit(solution)/shard_map/near/pallas_call | solution.py:479
  152.2 3.3 %far.1 = bf16[8,256,128]{2,1,0:T(8,128)(2,1)S(1)} custom-call(s32[2]{0:T(128)S(1)} %pad_add_fusion.where_ref.refs_0_, bf16[8,256,128]{2,1,0:T(8,128)(2,1)S(1)} %get-tuple-element.41.q_ref, f32[2048,128]{1,0:T(8,128)S(1)} %peaks.1.peak_ref, bf16[4,256,128]{2,1,0:T(8,128)(2,1)S(1)} %collective-permute-done.1.k2, ...), custom_call_target="tpu_custom_call" | custom-call | tf_op jit(solution)/shard_map/far/pallas_call | solution.py:487
  155.5 18.6 %all_to_all.10 = bf16[8,256,128]{2,1,0:T(8,128)(2,1)S(1)} all-to-all(bf16[8,256,128]{2,1,0:T(8,128)(2,1)S(1)} %far.1), channel_id=1, replica_groups={{0,32,64,96,128,160,192,224},{8,40,72,104,136,168,200,232},{16,48,80,11..., dimensions={0} | all-to-all | bytes 1048576 | tf_op jit(solution)/shard_map/all_to_all | solution.py:345
  174.1 0.2 copy.21
  174.3 1.0 copy.22
  (30 shorter events, 0.1 us)
Async XLA Ops:
  2.4 8.6 %copy-start.10 = (s32[256]{0:T(256)S(1)}, s32[256]{0:T(256)}, u32[]{:S(2)}) copy-start(s32[256]{0:T(256)} %param.14) | copy-start | bytes 3076
  2.4 102.1 %all-to-all-start = ((bf16[8,768,128]{2,1,0:T(8,128)(2,1)}), bf16[8,768,128]{2,1,0:T(8,128)(2,1)}, u32[]{:S(2)}, u32[]{:S(2)}) async-start(bf16[8,768,128]{2,1,0:T(8,128)(2,1)} %pack.1), calls=%async_computation | async-start | bytes 3145728 | tf_op jit(solution)/shard_map/all_to_all | solution.py:345
  11.0 6.8 %copy-start.9 = (bf16[64,7]{0,1:T(8,128)(2,1)S(1)}, bf16[64,7]{0,1:T(8,128)(2,1)}, u32[]{:S(2)}) copy-start(bf16[64,7]{0,1:T(8,128)(2,1)} %param.18) | copy-start | bytes 2692
  13.9 29.2 %collective-permute-start.4 = (bf16[8,1024]{1,0:T(8,128)(2,1)}, bf16[8,1024]{1,0:T(8,128)(2,1)S(1)}, u32[]{:S(2)}, u32[]{:S(2)}) collective-permute-start(bf16[8,1024]{1,0:T(8,128)(2,1)} %edge.1), channel_id=1, source_target_pairs={{0,8},{8,16},{16,24},{24,32},{32,40},{40,48},{48,56},{56,64},{64,7... | collective-permute-start | bytes 49160 | tf_op jit(solution)/shard_map/ppermute | solution.py:394
  17.9 37.3 %copy-start.6 = (f32[64,16]{0,1:T(8,128)S(1)}, f32[64,16]{0,1:T(8,128)}, u32[]{:S(2)}) copy-start(f32[64,16]{0,1:T(8,128)} %param.24) | copy-start | bytes 12292
  17.9 37.4 %copy-start.7 = (f32[64,16]{0,1:T(8,128)S(1)}, f32[64,16]{0,1:T(8,128)}, u32[]{:S(2)}) copy-start(f32[64,16]{0,1:T(8,128)} %param.25) | copy-start | bytes 12292
  17.9 37.5 %copy-start.5 = (bf16[64,128]{1,0:T(8,128)(2,1)S(1)}, bf16[64,128]{1,0:T(8,128)(2,1)}, u32[]{:S(2)}) copy-start(bf16[64,128]{1,0:T(8,128)(2,1)} %mr_ref.1) | copy-start | bytes 49156
  18.7 41.1 %copy-start = (bf16[256,1024]{1,0:T(8,128)(2,1)S(1)}, bf16[256,1024]{1,0:T(8,128)(2,1)}, u32[]{:S(2)}) copy-start(bf16[256,1024]{1,0:T(8,128)(2,1)} %liq_ref.1) | copy-start | bytes 1572868
  18.7 41.1 %copy-start.1 = (bf16[256,1024]{1,0:T(8,128)(2,1)S(1)}, bf16[256,1024]{1,0:T(8,128)(2,1)}, u32[]{:S(2)}) copy-start(bf16[256,1024]{1,0:T(8,128)(2,1)} %mrq_ref.1) | copy-start | bytes 1572868
  18.7 41.1 %copy-start.2 = (bf16[256,1024]{1,0:T(8,128)(2,1)S(1)}, bf16[256,1024]{1,0:T(8,128)(2,1)}, u32[]{:S(2)}) copy-start(bf16[256,1024]{1,0:T(8,128)(2,1)} %lik_ref.1) | copy-start | bytes 1572868
  43.1 0.6 copy-start.8
  48.7 11.1 %collective-permute-start.5 = (bf16[128,1024]{1,0:T(8,128)(2,1)}, bf16[128,1024]{1,0:T(8,128)(2,1)S(1)}, u32[]{:S(2)}, u32[]{:S(2)}) collective-permute-start(bf16[128,1024]{1,0:T(8,128)(2,1)} %get-tuple-element.25), channel_id=1, source_target_pairs={{0,8},{8,16},{16,24},{24,32},{32,40},{40,48},{48,56},{56,64},{64,7... | collective-permute-start | bytes 786440 | tf_op jit(solution)/shard_map/ppermute | solution.py:421
  59.8 1.0 copy-start.3
  60.9 1.0 copy-start.4
  71.4 12.8 %collective-permute-start.10 = (bf16[288,128]{1,0:T(8,128)(2,1)S(1)}, bf16[288,128]{1,0:T(8,128)(2,1)S(1)}, u32[]{:S(2)}, u32[]{:S(2)}) collective-permute-start(bf16[288,128]{1,0:T(8,128)(2,1)S(1)} %get-tuple-element.32), channel_id=1, source_target_pairs={{0,160},{8,168},{16,176},{24,184},{32,192},{40,200},{48,208},{56,2... | collective-permute-start | bytes 221192 | tf_op jit(solution)/shard_map/ppermute | solution.py:351
  71.5 16.5 %collective-permute-start.11 = (bf16[288,128]{1,0:T(8,128)(2,1)S(1)}, bf16[288,128]{1,0:T(8,128)(2,1)S(1)}, u32[]{:S(2)}, u32[]{:S(2)}) collective-permute-start(bf16[288,128]{1,0:T(8,128)(2,1)S(1)} %get-tuple-element.33), channel_id=1, source_target_pairs={{0,192},{8,200},{16,208},{24,216},{32,224},{40,232},{48,240},{56,2... | collective-permute-start | bytes 221192 | tf_op jit(solution)/shard_map/ppermute | solution.py:351
  80.6 10.5 %collective-permute-start.12 = (bf16[288,128]{1,0:T(8,128)(2,1)S(1)}, bf16[288,128]{1,0:T(8,128)(2,1)S(1)}, u32[]{:S(2)}, u32[]{:S(2)}) collective-permute-start(bf16[288,128]{1,0:T(8,128)(2,1)S(1)} %get-tuple-element.34), channel_id=1, source_target_pairs={{0,224},{8,232},{16,240},{24,248},{32,0},{40,8},{48,16},{56,24},{6... | collective-permute-start | bytes 221192 | tf_op jit(solution)/shard_map/ppermute | solution.py:351
  81.6 9.5 %collective-permute-start.6 = (bf16[288,128]{1,0:T(8,128)(2,1)S(1)}, bf16[288,128]{1,0:T(8,128)(2,1)S(1)}, u32[]{:S(2)}, u32[]{:S(2)}) collective-permute-start(bf16[288,128]{1,0:T(8,128)(2,1)S(1)} %get-tuple-element.28), channel_id=1, source_target_pairs={{0,32},{8,40},{16,48},{24,56},{32,64},{40,72},{48,80},{56,88},{64,... | collective-permute-start | bytes 221192 | tf_op jit(solution)/shard_map/ppermute | solution.py:351
  82.7 11.0 %collective-permute-start.7 = (bf16[288,128]{1,0:T(8,128)(2,1)S(1)}, bf16[288,128]{1,0:T(8,128)(2,1)S(1)}, u32[]{:S(2)}, u32[]{:S(2)}) collective-permute-start(bf16[288,128]{1,0:T(8,128)(2,1)S(1)} %get-tuple-element.29), channel_id=1, source_target_pairs={{0,64},{8,72},{16,80},{24,88},{32,96},{40,104},{48,112},{56,120},{... | collective-permute-start | bytes 221192 | tf_op jit(solution)/shard_map/ppermute | solution.py:351
  84.2 10.4 %collective-permute-start.8 = (bf16[288,128]{1,0:T(8,128)(2,1)S(1)}, bf16[288,128]{1,0:T(8,128)(2,1)S(1)}, u32[]{:S(2)}, u32[]{:S(2)}) collective-permute-start(bf16[288,128]{1,0:T(8,128)(2,1)S(1)} %get-tuple-element.30), channel_id=1, source_target_pairs={{0,96},{8,104},{16,112},{24,120},{32,128},{40,136},{48,144},{56,15... | collective-permute-start | bytes 221192 | tf_op jit(solution)/shard_map/ppermute | solution.py:351
  88.0 8.7 %collective-permute-start.9 = (bf16[288,128]{1,0:T(8,128)(2,1)S(1)}, bf16[288,128]{1,0:T(8,128)(2,1)S(1)}, u32[]{:S(2)}, u32[]{:S(2)}) collective-permute-start(bf16[288,128]{1,0:T(8,128)(2,1)S(1)} %get-tuple-element.31), channel_id=1, source_target_pairs={{0,128},{8,136},{16,144},{24,152},{32,160},{40,168},{48,176},{56,1... | collective-permute-start | bytes 221192 | tf_op jit(solution)/shard_map/ppermute | solution.py:351
  97.3 11.7 %collective-permute-start.13 = (bf16[8,32,128]{2,1,0:T(8,128)(2,1)S(1)}, bf16[8,32,128]{2,1,0:T(8,128)(2,1)S(1)}, u32[]{:S(2)}, u32[]{:S(2)}) collective-permute-start(bf16[8,32,128]{2,1,0:T(8,128)(2,1)S(1)} %get-tuple-element.36.refs_2_), channel_id=1, source_target_pairs={{0,8},{8,16},{16,24},{24,0},{32,40},{40,48},{48,56},{56,32},{64,72... | collective-permute-start | bytes 196616 | tf_op jit(solution)/shard_map/ppermute | solution.py:444
  103.6 6.5 %collective-permute-start.14 = (bf16[8,32,128]{2,1,0:T(8,128)(2,1)S(1)}, bf16[8,32,128]{2,1,0:T(8,128)(2,1)S(1)}, u32[]{:S(2)}, u32[]{:S(2)}) collective-permute-start(bf16[8,32,128]{2,1,0:T(8,128)(2,1)S(1)} %get-tuple-element.36.refs_2_), channel_id=1, source_target_pairs={{0,16},{8,24},{16,0},{24,8},{32,48},{40,56},{48,32},{56,40},{64,80... | collective-permute-start | bytes 196616 | tf_op jit(solution)/shard_map/ppermute | solution.py:444
  103.6 6.9 %collective-permute-start.15 = (bf16[8,32,128]{2,1,0:T(8,128)(2,1)S(1)}, bf16[8,32,128]{2,1,0:T(8,128)(2,1)S(1)}, u32[]{:S(2)}, u32[]{:S(2)}) collective-permute-start(bf16[8,32,128]{2,1,0:T(8,128)(2,1)S(1)} %get-tuple-element.36.refs_2_), channel_id=1, source_target_pairs={{0,24},{8,0},{16,8},{24,16},{32,56},{40,32},{48,40},{56,48},{64,88... | collective-permute-start | bytes 196616 | tf_op jit(solution)/shard_map/ppermute | solution.py:444
  106.0 15.4 %collective-permute-start = (bf16[8,256,128]{2,1,0:T(8,128)(2,1)S(1)}, bf16[8,256,128]{2,1,0:T(8,128)(2,1)S(1)}, u32[]{:S(2)}, u32[]{:S(2)}) collective-permute-start(bf16[8,256,128]{2,1,0:T(8,128)(2,1)S(1)} %get-tuple-element.40.k0), channel_id=1, source_target_pairs={{0,8},{8,16},{16,24},{24,0},{32,40},{40,48},{48,56},{56,32},{64,72... | collective-permute-start | bytes 1572872 | tf_op jit(solution)/shard_map/ppermute | solution.py:359
  108.4 16.1 %collective-permute-start.2 = (bf16[8,256,128]{2,1,0:T(8,128)(2,1)S(1)}, bf16[8,256,128]{2,1,0:T(8,128)(2,1)S(1)}, u32[]{:S(2)}, u32[]{:S(2)}) collective-permute-start(bf16[8,256,128]{2,1,0:T(8,128)(2,1)S(1)} %get-tuple-element.40.k0), channel_id=1, source_target_pairs={{0,24},{8,0},{16,8},{24,16},{32,56},{40,32},{48,40},{56,48},{64,88... | collective-permute-start | bytes 1572872 | tf_op jit(solution)/shard_map/ppermute | solution.py:360
  113.1 18.7 %collective-permute-start.16 = (bf16[8,256,128]{2,1,0:T(8,128)(2,1)S(1)}, bf16[8,256,128]{2,1,0:T(8,128)(2,1)S(1)}, u32[]{:S(2)}, u32[]{:S(2)}) collective-permute-start(bf16[8,256,128]{2,1,0:T(8,128)(2,1)S(1)} %values.1.v0), channel_id=1, source_target_pairs={{0,8},{8,16},{16,24},{24,0},{32,40},{40,48},{48,56},{56,32},{64,72... | collective-permute-start | bytes 1572872 | tf_op jit(solution)/shard_map/ppermute | solution.py:359
  114.7 20.9 %collective-permute-start.18 = (bf16[8,256,128]{2,1,0:T(8,128)(2,1)S(1)}, bf16[8,256,128]{2,1,0:T(8,128)(2,1)S(1)}, u32[]{:S(2)}, u32[]{:S(2)}) collective-permute-start(bf16[8,256,128]{2,1,0:T(8,128)(2,1)S(1)} %values.1.v0), channel_id=1, source_target_pairs={{0,24},{8,0},{16,8},{24,16},{32,56},{40,32},{48,40},{56,48},{64,88... | collective-permute-start | bytes 1572872 | tf_op jit(solution)/shard_map/ppermute | solution.py:360
  121.4 14.2 %collective-permute-start.1 = (bf16[4,256,128]{2,1,0:T(8,128)(2,1)S(1)}, bf16[4,256,128]{2,1,0:T(8,128)(2,1)S(1)}, u32[]{:S(2)}, u32[]{:S(2)}) collective-permute-start(bf16[4,256,128]{2,1,0:T(8,128)(2,1)S(1)} %slice.30), channel_id=1, source_target_pairs={{0,8},{8,16},{16,24},{24,0},{32,40},{40,48},{48,56},{56,32},{64,72... | collective-permute-start | bytes 786440 | tf_op jit(solution)/shard_map/ppermute | solution.py:363
  124.5 13.5 %collective-permute-start.3 = (bf16[4,256,128]{2,1,0:T(8,128)(2,1)S(1)}, bf16[4,256,128]{2,1,0:T(8,128)(2,1)S(1)}, u32[]{:S(2)}, u32[]{:S(2)}) collective-permute-start(bf16[4,256,128]{2,1,0:T(8,128)(2,1)S(1)} %slice.31), channel_id=1, source_target_pairs={{0,24},{8,0},{16,8},{24,16},{32,56},{40,32},{48,40},{56,48},{64,88... | collective-permute-start | bytes 786440 | tf_op jit(solution)/shard_map/ppermute | solution.py:364
  131.8 20.3 %collective-permute-start.17 = (bf16[4,256,128]{2,1,0:T(8,128)(2,1)S(1)}, bf16[4,256,128]{2,1,0:T(8,128)(2,1)S(1)}, u32[]{:S(2)}, u32[]{:S(2)}) collective-permute-start(bf16[4,256,128]{2,1,0:T(8,128)(2,1)S(1)} %slice.33), channel_id=1, source_target_pairs={{0,8},{8,16},{16,24},{24,0},{32,40},{40,48},{48,56},{56,32},{64,72... | collective-permute-start | bytes 786440 | tf_op jit(solution)/shard_map/ppermute | solution.py:363
  135.6 16.6 %collective-permute-start.19 = (bf16[4,256,128]{2,1,0:T(8,128)(2,1)S(1)}, bf16[4,256,128]{2,1,0:T(8,128)(2,1)S(1)}, u32[]{:S(2)}, u32[]{:S(2)}) collective-permute-start(bf16[4,256,128]{2,1,0:T(8,128)(2,1)S(1)} %slice.34), channel_id=1, source_target_pairs={{0,24},{8,0},{16,8},{24,16},{32,56},{40,32},{48,40},{56,48},{64,88... | collective-permute-start | bytes 786440 | tf_op jit(solution)/shard_map/ppermute | solution.py:364

commit v3 on v2

--- a/solution.py
+++ b/solution.py
@@ -169,13 +169,13 @@
             for (low, high), out_ref in zip(bounds, refs[count:]):
                 out_ref[z] = refs[s][low:high, :]
 
-    inside = pl.BlockSpec(memory_space=pltpu.VMEM)
+    sizes = [(count, high - low, LANES) for low, high in bounds]
     return pl.pallas_call(
         body,
-        in_specs=[pl.BlockSpec(memory_space=pltpu.SMEM)] + [inside] * count,
-        out_specs=[inside] * len(cuts),
-        out_shape=[jax.ShapeDtypeStruct((count, high - low, LANES), BF16) for low, high in bounds],
-        compiler_params=pltpu.CompilerParams(vmem_limit_bytes=16 * MIB),
+        grid=(1,),
+        in_specs=[pl.BlockSpec(memory_space=pltpu.SMEM)] + [whole((cuts[-1], LANES))] * count,
+        out_specs=[whole(size) for size in sizes],
+        out_shape=[jax.ShapeDtypeStruct(size, BF16) for size in sizes],
     )(where, *parts)
 
 

time: 176 us -> 179 us (1.017)
  the two profiles are of different devices: /device:TPU:6 before, /device:TPU:10 now
where the time goes in v3:
time: 179 us; the launch traced here: 178 us
  starting transfers between devices  75.9 us (42%)
  Pallas kernels  45 us (25%)
  waiting for transfers between devices  28.7 us (16%)
  blocking collectives  19 us (11%)
  local copies, waits for them, and re-layouts  8.95 us (5%)
    ppermute x7, starting transfers between devices, shifted(): lax.ppermute(part, 'seq', [(d, (d // STRIPE + s) % depth * STRIPE + d % S...  44.8 us
    all_to_all x1, blocking collectives, exchange(): lax.all_to_all(packed, 'seq', split_axis=0, concat_axis=0, tiled=True, ax...  19 us
    ppermute x2, waiting for transfers between devices, spread(): behind = lax.ppermute(part, 'seq', turn(1))  15.1 us
    pallas_call x1, Pallas kernels, local(): pl.pallas_call(conv_kernel, grid_spec=pltpu.PrefetchScalarGridSpec(num_sc...  9.47 us
    all_to_all x1, starting transfers between devices, exchange(): lax.all_to_all(packed, 'seq', split_axis=0, concat_axis=0, tiled=True, ax...  8.6 us
    pallas_call x1, Pallas kernels, local(): pl.pallas_call(near_kernel, in_specs=[smem] + [inside] * 8, out_specs=[in...  8.49 us
    ppermute x7, waiting for transfers between devices, shifted(): lax.ppermute(part, 'seq', [(d, (d // STRIPE + s) % depth * STRIPE + d % S...  7.07 us
    ppermute x3, starting transfers between devices, local(): others = [lax.ppermute(states, 'seq', turn(k)) for k in range(1, STRIPE)]  6.55 us
  transfers between devices with their start and end apart: 21, of which 11 were waited for; matrix products, arithmetic and copies ran while one was open for 2% of the time, Pallas kernels for 22%

profile of v3, /device:TPU:10, one launch (start us, length us, event | category | flops | bytes accessed | tf_op | source)
XLA Modules:
  0.0 178.0 jit_solution(10797810097495594192)
XLA Ops:
  0.0 2.4 %pack.1 = bf16[8,768,128]{2,1,0:T(8,128)(2,1)} custom-call(bf16[256,1024]{1,0:T(8,128)(2,1)} %a_ref.1, bf16[256,1024]{1,0:T(8,128)(2,1)} %b_ref.1, bf16[256,1024]{1,0:T(8,128)(2,1)} %liq_ref.1), custom_call_target="tpu_custom_call" | custom-call | tf_op jit(solution)/shard_map/pack/pallas_call | solution.py:370
  2.4 8.6 %all-to-all-start = ((bf16[8,768,128]{2,1,0:T(8,128)(2,1)}), bf16[8,768,128]{2,1,0:T(8,128)(2,1)}, u32[]{:S(2)}, u32[]{:S(2)}) async-start(bf16[8,768,128]{2,1,0:T(8,128)(2,1)} %pack.1), calls=%async_computation | async-start | bytes 3145728 | tf_op jit(solution)/shard_map/all_to_all | solution.py:345
  11.0 0.8 copy.20.tok_ref
  11.8 2.1 %edge.1 = bf16[8,1024]{1,0:T(8,128)(2,1)} custom-call(s32[256,1]{1,0:T(8,128)} %copy.20.tok_ref, bf16[512,1024]{1,0:T(8,128)(2,1)} %table_ref.3, bf16[256,1024]{1,0:T(8,128)(2,1)} %key_ref.3), custom_call_target="tpu_custom_call" | custom-call | tf_op jit(solution)/shard_map/edge/pallas_call | solution.py:382
  13.9 3.4 %collective-permute-start.4 = (bf16[8,1024]{1,0:T(8,128)(2,1)}, bf16[8,1024]{1,0:T(8,128)(2,1)S(1)}, u32[]{:S(2)}, u32[]{:S(2)}) collective-permute-start(bf16[8,1024]{1,0:T(8,128)(2,1)} %edge.1), channel_id=1, source_target_pairs={{0,8},{8,16},{16,24},{24,32},{32,40},{40,48},{48,56},{56,64},{64,7... | collective-permute-start | bytes 49160 | tf_op jit(solution)/shard_map/ppermute | solution.py:394
  17.3 0.1 broadcast_in_dim.9
  17.4 0.0 copy-start.18
  17.5 0.0 copy-start.19
  17.5 0.0 copy-start.10
  17.5 0.7 reshape.15.filt_ref
  18.2 1.5 collective-permute-done.4.edge_ref
  19.7 0.6 copy-done.20
  20.3 5.0 %short.1 = (bf16[256,1024]{1,0:T(8,128)(2,1)}, bf16[256,1024]{1,0:T(8,128)(2,1)}, bf16[128,1024]{1,0:T(8,128)(2,1)}) custom-call(s32[256,1]{1,0:T(8,128)} %copy.20.tok_ref, bf16[512,1024]{1,0:T(8,128)(2,1)} %table_ref.3, bf16[8,1024]{1,0:T(8,128)(2,1)} %copy-done.20, bf16[256,1024]{1,0:T(8,128)(2,1)} %query_ref.1, bf16[256,1024]{1,0:T(8,128)(2,1)} %key_ref.3, ...), custom_call_target="tpu_custom_call" | custom-call | tf_op jit(solution)/shard_map/short/pallas_call | solution.py:404
  25.4 3.4 %collective-permute-start.5 = (bf16[128,1024]{1,0:T(8,128)(2,1)}, bf16[128,1024]{1,0:T(8,128)(2,1)S(1)}, u32[]{:S(2)}, u32[]{:S(2)}) collective-permute-start(bf16[128,1024]{1,0:T(8,128)(2,1)} %get-tuple-element.25), channel_id=1, source_target_pairs={{0,8},{8,16},{16,24},{24,32},{32,40},{40,48},{48,56},{56,64},{64,7... | collective-permute-start | bytes 786440 | tf_op jit(solution)/shard_map/ppermute | solution.py:421
  28.8 0.1 copy.17.rate_ref
  28.9 0.1 copy.18.res_ref
  29.0 3.9 %tables.1 = (bf16[8,1024,256]{2,1,0:T(8,128)(2,1)S(1)}, bf16[8,1152,256]{2,1,0:T(8,128)(2,1)S(1)}) custom-call(bf16[64,128]{1,0:T(8,128)(2,1)S(1)} %copy-done.10, f32[64,16]{1,0:T(8,128)S(1)} %copy.17.rate_ref, f32[64,16]{1,0:T(8,128)S(1)} %copy.18.res_ref), custom_call_target="tpu_custom_call" | custom-call | tf_op jit(solution)/shard_map/tables/pallas_call | solution.py:62
  32.9 0.1 pad_add_fusion.where_ref.refs_0_
  33.0 1.5 collective-permute-done.5.halo_ref
  34.5 1.0 copy-done.3
  35.5 1.0 copy-done.4
  36.6 9.5 %medium_long.1 = (bf16[288,128]{1,0:T(8,128)(2,1)S(1)}, bf16[288,128]{1,0:T(8,128)(2,1)S(1)}, bf16[288,128]{1,0:T(8,128)(2,1)S(1)}, bf16[288,128]{1,0:T(8,128)(2...) custom-call(s32[2]{0:T(128)S(1)} %pad_add_fusion.where_ref.refs_0_, ...), custom_call_target="tpu_custom_call" | custom-call | tf_op jit(solution)/shard_map/medium_long/pallas_call | solution.py:427
  46.1 0.6 copy-done.6
  46.7 34.3 %collective-permute-start.10 = (bf16[288,128]{1,0:T(8,128)(2,1)S(1)}, bf16[288,128]{1,0:T(8,128)(2,1)S(1)}, u32[]{:S(2)}, u32[]{:S(2)}) collective-permute-start(bf16[288,128]{1,0:T(8,128)(2,1)S(1)} %get-tuple-element.32), channel_id=1, source_target_pairs={{0,160},{8,168},{16,176},{24,184},{32,192},{40,200},{48,208},{56,2... | collective-permute-start | bytes 221192 | tf_op jit(solution)/shard_map/ppermute | solution.py:351
  81.0 0.3 collective-permute-start.11
  81.4 0.2 collective-permute-start.12
  81.6 1.8 %collective-permute-start.6 = (bf16[288,128]{1,0:T(8,128)(2,1)S(1)}, bf16[288,128]{1,0:T(8,128)(2,1)S(1)}, u32[]{:S(2)}, u32[]{:S(2)}) collective-permute-start(bf16[288,128]{1,0:T(8,128)(2,1)S(1)} %get-tuple-element.28), channel_id=1, source_target_pairs={{0,32},{8,40},{16,48},{24,56},{32,64},{40,72},{48,80},{56,88},{64,... | collective-permute-start | bytes 221192 | tf_op jit(solution)/shard_map/ppermute | solution.py:351
  83.4 2.6 %collective-permute-start.7 = (bf16[288,128]{1,0:T(8,128)(2,1)S(1)}, bf16[288,128]{1,0:T(8,128)(2,1)S(1)}, u32[]{:S(2)}, u32[]{:S(2)}) collective-permute-start(bf16[288,128]{1,0:T(8,128)(2,1)S(1)} %get-tuple-element.29), channel_id=1, source_target_pairs={{0,64},{8,72},{16,80},{24,88},{32,96},{40,104},{48,112},{56,120},{... | collective-permute-start | bytes 221192 | tf_op jit(solution)/shard_map/ppermute | solution.py:351
  86.0 3.6 %collective-permute-start.8 = (bf16[288,128]{1,0:T(8,128)(2,1)S(1)}, bf16[288,128]{1,0:T(8,128)(2,1)S(1)}, u32[]{:S(2)}, u32[]{:S(2)}) collective-permute-start(bf16[288,128]{1,0:T(8,128)(2,1)S(1)} %get-tuple-element.30), channel_id=1, source_target_pairs={{0,96},{8,104},{16,112},{24,120},{32,128},{40,136},{48,144},{56,15... | collective-permute-start | bytes 221192 | tf_op jit(solution)/shard_map/ppermute | solution.py:351
  89.6 2.0 %collective-permute-start.9 = (bf16[288,128]{1,0:T(8,128)(2,1)S(1)}, bf16[288,128]{1,0:T(8,128)(2,1)S(1)}, u32[]{:S(2)}, u32[]{:S(2)}) collective-permute-start(bf16[288,128]{1,0:T(8,128)(2,1)S(1)} %get-tuple-element.31), channel_id=1, source_target_pairs={{0,128},{8,136},{16,144},{24,152},{32,160},{40,168},{48,176},{56,1... | collective-permute-start | bytes 221192 | tf_op jit(solution)/shard_map/ppermute | solution.py:351
  91.5 0.1 dynamic-slice_bitcast_fusion
  91.6 0.1 broadcast_in_dim.10
  91.7 0.1 reshape.16.refs_7_
  91.8 0.1 broadcast_in_dim.11
  91.8 0.1 reshape.17.refs_8_
  92.0 1.2 collective-permute-done.7.refs_2_
  93.2 2.3 %collective-permute-done.8.refs_3_ = bf16[288,128]{1,0:T(8,128)(2,1)S(1)} collective-permute-done((bf16[288,128]{1,0:T(8,128)(2,1)S(1)}, bf16[288,128]{1,0:T(8,128)(2,1)S(1)}, u32[]{:S(2)}, u32[]{:S(2)}) %collective-permute-start.8) | collective-permute-done | bytes 73760 | tf_op jit(solution)/shard_map/ppermute | solution.py:351
  95.5 3.6 %collective-permute-done.9.refs_4_ = bf16[288,128]{1,0:T(8,128)(2,1)S(1)} collective-permute-done((bf16[288,128]{1,0:T(8,128)(2,1)S(1)}, bf16[288,128]{1,0:T(8,128)(2,1)S(1)}, u32[]{:S(2)}, u32[]{:S(2)}) %collective-permute-start.9) | collective-permute-done | bytes 73760 | tf_op jit(solution)/shard_map/ppermute | solution.py:351
  99.1 0.6 copy-done.17
  99.7 2.0 %shard_map.136 = (bf16[8,256,128]{2,1,0:T(8,128)(2,1)}, bf16[8,32,128]{2,1,0:T(8,128)(2,1)}) custom-call(s32[2]{0:T(128)} %copy-done.8, bf16[288,128]{1,0:T(8,128)(2,1)} %copy-done.6, bf16[288,128]{1,0:T(8,128)(2,1)} %copy-done.14, bf16[288,128]{1,0:T(8,128)(2,1)} %copy-done.15, bf16[288,128]{1,0:T(8,128)(2,1)} %copy-done.16, bf16[288,128]{1,0:T(8,128)(2,1)} %copy-done.17, ...), custom_call_target="tpu_custom_call" | custom-call | tf_op jit(solution)/shard_map/pallas_call | solution.py:173
  101.7 0.1 collective-permute-start.13
  101.7 6.5 %collective-permute-start.14 = (bf16[8,32,128]{2,1,0:T(8,128)(2,1)}, bf16[8,32,128]{2,1,0:T(8,128)(2,1)S(1)}, u32[]{:S(2)}, u32[]{:S(2)}) collective-permute-start(bf16[8,32,128]{2,1,0:T(8,128)(2,1)} %get-tuple-element.36.refs_2_), channel_id=1, source_target_pairs={{0,16},{8,24},{16,0},{24,8},{32,48},{40,56},{48,32},{56,40},{64,80... | collective-permute-start | bytes 196616 | tf_op jit(solution)/shard_map/ppermute | solution.py:444
  108.2 1.5 fusion
  109.7 2.1 %collective-permute-start = (bf16[8,256,128]{2,1,0:T(8,128)(2,1)S(1)}, bf16[8,256,128]{2,1,0:T(8,128)(2,1)S(1)}, u32[]{:S(2)}, u32[]{:S(2)}) collective-permute-start(bf16[8,256,128]{2,1,0:T(8,128)(2,1)S(1)} %get-tuple-element.40.k0), channel_id=1, source_target_pairs={{0,8},{8,16},{16,24},{24,0},{32,40},{40,48},{48,56},{56,32},{64,72... | collective-permute-start | bytes 1572872 | tf_op jit(solution)/shard_map/ppermute | solution.py:359
  111.8 0.0 collective-permute-start.2
  111.8 1.5 collective-permute-done.15.refs_6_
  113.4 2.6 %values.1.v0 = bf16[8,256,128]{2,1,0:T(8,128)(2,1)S(1)} custom-call(s32[2]{0:T(128)S(1)} %copy-done.9, bf16[8,256,128]{2,1,0:T(8,128)(2,1)S(1)} %copy-done.5, bf16[8,32,128]{2,1,0:T(8,128)(2,1)S(1)} %copy-done.7, bf16[8,256,128]{2,1,0:T(8,128)(2,1)S(1)} %get-tuple-element.39.refs_3_, bf16[8,32,128]{2,1,0:T(8,128)(2,1)S(1)} %collective-permute-done.13.refs_4_, ...), custom_call_target="tpu_custom_call" | custom-call | tf_op jit(solution)/shard_map/values/pallas_call | solution.py:455
  116.0 0.6 collective-permute-start.16
  116.6 1.5 collective-permute-start.18
  118.1 6.5 %collective-permute-done.k1 = bf16[8,256,128]{2,1,0:T(8,128)(2,1)S(1)} collective-permute-done((bf16[8,256,128]{2,1,0:T(8,128)(2,1)S(1)}, bf16[8,256,128]{2,1,0:T(8,128)(2,1)S(1)}, u32[]{:S(2)}, u32[]{:S(2)}) %collective-permute-start) | collective-permute-done | bytes 524320 | tf_op jit(solution)/shard_map/ppermute | solution.py:359
  124.6 2.1 %collective-permute-start.1 = (bf16[4,256,128]{2,1,0:T(8,128)(2,1)S(1)}, bf16[4,256,128]{2,1,0:T(8,128)(2,1)S(1)}, u32[]{:S(2)}, u32[]{:S(2)}) collective-permute-start(bf16[4,256,128]{2,1,0:T(8,128)(2,1)S(1)} %slice.30), channel_id=1, source_target_pairs={{0,8},{8,16},{16,24},{24,0},{32,40},{40,48},{48,56},{56,32},{64,72... | collective-permute-start | bytes 786440 | tf_op jit(solution)/shard_map/ppermute | solution.py:363
  126.7 0.5 collective-permute-start.3
  127.2 8.6 %collective-permute-done.16.v1 = bf16[8,256,128]{2,1,0:T(8,128)(2,1)S(1)} collective-permute-done((bf16[8,256,128]{2,1,0:T(8,128)(2,1)S(1)}, bf16[8,256,128]{2,1,0:T(8,128)(2,1)S(1)}, u32[]{:S(2)}, u32[]{:S(2)}) %collective-permute-start.16) | collective-permute-done | bytes 524320 | tf_op jit(solution)/shard_map/ppermute | solution.py:359
  135.9 1.3 collective-permute-start.17
  137.1 0.3 collective-permute-done.18.v4
  137.5 1.2 collective-permute-start.19
  138.7 0.2 collective-permute-done.1.k2
  138.8 1.5 collective-permute-done.3.k3
  140.3 5.7 %peaks.1.peak_ref = f32[2048,128]{1,0:T(8,128)S(1)} custom-call(s32[2]{0:T(128)S(1)} %copy-done.9, bf16[8,256,128]{2,1,0:T(8,128)(2,1)S(1)} %get-tuple-element.41.q_ref, bf16[8,256,128]{2,1,0:T(8,128)(2,1)S(1)} %get-tuple-element.40.k0, bf16[8,256,128]{2,1,0:T(8,128)(2,1)S(1)} %collective-permute-done.k1, ...), custom_call_target="tpu_custom_call" | custom-call | tf_op jit(solution)/shard_map/peaks/pallas_call | solution.py:467
  146.0 8.5 %near.1 = (f32[2048,128]{1,0:T(8,128)S(1)}, f32[2048,128]{1,0:T(8,128)S(1)}) custom-call(s32[2]{0:T(128)S(1)} %copy-done.9, bf16[8,256,128]{2,1,0:T(8,128)(2,1)S(1)} %get-tuple-element.41.q_ref, f32[2048,128]{1,0:T(8,128)S(1)} %peaks.1.peak_ref, bf16[8,256,128]{2,1,0:T(8,128)(2,1)S(1)} %get-tuple-element.40.k0, ...), custom_call_target="tpu_custom_call" | custom-call | tf_op jit(solution)/shard_map/near/pallas_call | solution.py:479
  154.5 3.3 %far.1 = bf16[8,256,128]{2,1,0:T(8,128)(2,1)S(1)} custom-call(s32[2]{0:T(128)S(1)} %copy-done.9, bf16[8,256,128]{2,1,0:T(8,128)(2,1)S(1)} %get-tuple-element.41.q_ref, f32[2048,128]{1,0:T(8,128)S(1)} %peaks.1.peak_ref, bf16[4,256,128]{2,1,0:T(8,128)(2,1)S(1)} %collective-permute-done.1.k2, bf16[4,256,128]{2,1,0:T(8,128)(2,1)S(1)} %collective-permute-done.3.k3, ...), custom_call_target="tpu_custom_call" | custom-call | tf_op jit(solution)/shard_map/far/pallas_call | solution.py:487
  157.8 19.0 %all_to_all.10 = bf16[8,256,128]{2,1,0:T(8,128)(2,1)S(1)} all-to-all(bf16[8,256,128]{2,1,0:T(8,128)(2,1)S(1)} %far.1), channel_id=1, replica_groups={{0,32,64,96,128,160,192,224},{8,40,72,104,136,168,200,232},{16,48,80,11..., dimensions={0} | all-to-all | bytes 1048576 | tf_op jit(solution)/shard_map/all_to_all | solution.py:345
  176.8 0.2 copy.21
  177.0 1.0 copy.22
  (54 shorter events, 0.2 us)
Async XLA Ops:
  2.4 8.6 %copy-start.22 = (s32[256]{0:T(256)S(1)}, s32[256]{0:T(256)}, u32[]{:S(2)}) copy-start(s32[256]{0:T(256)} %param.14) | copy-start | bytes 3076
  2.4 105.8 %all-to-all-start = ((bf16[8,768,128]{2,1,0:T(8,128)(2,1)}), bf16[8,768,128]{2,1,0:T(8,128)(2,1)}, u32[]{:S(2)}, u32[]{:S(2)}) async-start(bf16[8,768,128]{2,1,0:T(8,128)(2,1)} %pack.1), calls=%async_computation | async-start | bytes 3145728 | tf_op jit(solution)/shard_map/all_to_all | solution.py:345
  11.0 6.3 %copy-start.21 = (bf16[64,7]{0,1:T(8,128)(2,1)S(1)}, bf16[64,7]{0,1:T(8,128)(2,1)}, u32[]{:S(2)}) copy-start(bf16[64,7]{0,1:T(8,128)(2,1)} %param.18) | copy-start | bytes 2692
  13.9 5.8 %collective-permute-start.4 = (bf16[8,1024]{1,0:T(8,128)(2,1)}, bf16[8,1024]{1,0:T(8,128)(2,1)S(1)}, u32[]{:S(2)}, u32[]{:S(2)}) collective-permute-start(bf16[8,1024]{1,0:T(8,128)(2,1)} %edge.1), channel_id=1, source_target_pairs={{0,8},{8,16},{16,24},{24,32},{32,40},{40,48},{48,56},{56,64},{64,7... | collective-permute-start | bytes 49160 | tf_op jit(solution)/shard_map/ppermute | solution.py:394
  17.4 11.3 %copy-start.18 = (f32[64,16]{0,1:T(8,128)S(1)}, f32[64,16]{0,1:T(8,128)}, u32[]{:S(2)}) copy-start(f32[64,16]{0,1:T(8,128)} %param.24) | copy-start | bytes 12292
  17.5 11.4 %copy-start.19 = (f32[64,16]{0,1:T(8,128)S(1)}, f32[64,16]{0,1:T(8,128)}, u32[]{:S(2)}) copy-start(f32[64,16]{0,1:T(8,128)} %param.25) | copy-start | bytes 12292
  17.5 11.5 %copy-start.10 = (bf16[64,128]{1,0:T(8,128)(2,1)S(1)}, bf16[64,128]{1,0:T(8,128)(2,1)}, u32[]{:S(2)}) copy-start(bf16[64,128]{1,0:T(8,128)(2,1)} %mr_ref.1) | copy-start | bytes 49156
  18.2 16.3 %copy-start = (bf16[256,1024]{1,0:T(8,128)(2,1)S(1)}, bf16[256,1024]{1,0:T(8,128)(2,1)}, u32[]{:S(2)}) copy-start(bf16[256,1024]{1,0:T(8,128)(2,1)} %liq_ref.1) | copy-start | bytes 1572868
  18.2 16.3 %copy-start.1 = (bf16[256,1024]{1,0:T(8,128)(2,1)S(1)}, bf16[256,1024]{1,0:T(8,128)(2,1)}, u32[]{:S(2)}) copy-start(bf16[256,1024]{1,0:T(8,128)(2,1)} %mrq_ref.1) | copy-start | bytes 1572868
  18.2 16.3 %copy-start.2 = (bf16[256,1024]{1,0:T(8,128)(2,1)S(1)}, bf16[256,1024]{1,0:T(8,128)(2,1)}, u32[]{:S(2)}) copy-start(bf16[256,1024]{1,0:T(8,128)(2,1)} %lik_ref.1) | copy-start | bytes 1572868
  19.7 0.6 copy-start.20
  25.4 9.1 %collective-permute-start.5 = (bf16[128,1024]{1,0:T(8,128)(2,1)}, bf16[128,1024]{1,0:T(8,128)(2,1)S(1)}, u32[]{:S(2)}, u32[]{:S(2)}) collective-permute-start(bf16[128,1024]{1,0:T(8,128)(2,1)} %get-tuple-element.25), channel_id=1, source_target_pairs={{0,8},{8,16},{16,24},{24,32},{32,40},{40,48},{48,56},{56,64},{64,7... | collective-permute-start | bytes 786440 | tf_op jit(solution)/shard_map/ppermute | solution.py:421
  33.0 13.1 %copy-start.8 = (s32[2]{0:T(128)}, s32[2]{0:T(128)S(1)}, u32[]{:S(2)}) copy-start(s32[2]{0:T(128)S(1)} %pad_add_fusion.where_ref.refs_0_) | copy-start | bytes 28
  34.5 1.0 copy-start.3
  35.5 1.0 copy-start.4
  46.1 0.6 copy-start.6
  46.7 39.3 %collective-permute-start.10 = (bf16[288,128]{1,0:T(8,128)(2,1)S(1)}, bf16[288,128]{1,0:T(8,128)(2,1)S(1)}, u32[]{:S(2)}, u32[]{:S(2)}) collective-permute-start(bf16[288,128]{1,0:T(8,128)(2,1)S(1)} %get-tuple-element.32), channel_id=1, source_target_pairs={{0,160},{8,168},{16,176},{24,184},{32,192},{40,200},{48,208},{56,2... | collective-permute-start | bytes 221192 | tf_op jit(solution)/shard_map/ppermute | solution.py:351
  81.0 8.5 %collective-permute-start.11 = (bf16[288,128]{1,0:T(8,128)(2,1)S(1)}, bf16[288,128]{1,0:T(8,128)(2,1)S(1)}, u32[]{:S(2)}, u32[]{:S(2)}) collective-permute-start(bf16[288,128]{1,0:T(8,128)(2,1)S(1)} %get-tuple-element.33), channel_id=1, source_target_pairs={{0,192},{8,200},{16,208},{24,216},{32,224},{40,232},{48,240},{56,2... | collective-permute-start | bytes 221192 | tf_op jit(solution)/shard_map/ppermute | solution.py:351
  81.4 10.6 %collective-permute-start.12 = (bf16[288,128]{1,0:T(8,128)(2,1)S(1)}, bf16[288,128]{1,0:T(8,128)(2,1)S(1)}, u32[]{:S(2)}, u32[]{:S(2)}) collective-permute-start(bf16[288,128]{1,0:T(8,128)(2,1)S(1)} %get-tuple-element.34), channel_id=1, source_target_pairs={{0,224},{8,232},{16,240},{24,248},{32,0},{40,8},{48,16},{56,24},{6... | collective-permute-start | bytes 221192 | tf_op jit(solution)/shard_map/ppermute | solution.py:351
  81.6 10.3 %collective-permute-start.6 = (bf16[288,128]{1,0:T(8,128)(2,1)S(1)}, bf16[288,128]{1,0:T(8,128)(2,1)S(1)}, u32[]{:S(2)}, u32[]{:S(2)}) collective-permute-start(bf16[288,128]{1,0:T(8,128)(2,1)S(1)} %get-tuple-element.28), channel_id=1, source_target_pairs={{0,32},{8,40},{16,48},{24,56},{32,64},{40,72},{48,80},{56,88},{64,... | collective-permute-start | bytes 221192 | tf_op jit(solution)/shard_map/ppermute | solution.py:351
  83.4 9.8 %collective-permute-start.7 = (bf16[288,128]{1,0:T(8,128)(2,1)S(1)}, bf16[288,128]{1,0:T(8,128)(2,1)S(1)}, u32[]{:S(2)}, u32[]{:S(2)}) collective-permute-start(bf16[288,128]{1,0:T(8,128)(2,1)S(1)} %get-tuple-element.29), channel_id=1, source_target_pairs={{0,64},{8,72},{16,80},{24,88},{32,96},{40,104},{48,112},{56,120},{... | collective-permute-start | bytes 221192 | tf_op jit(solution)/shard_map/ppermute | solution.py:351
  86.0 13.0 %copy-start.11 = (bf16[288,128]{1,0:T(8,128)(2,1)}, bf16[288,128]{1,0:T(8,128)(2,1)S(1)}, u32[]{:S(2)}) copy-start(bf16[288,128]{1,0:T(8,128)(2,1)S(1)} %collective-permute-done.10.refs_5_) | copy-start | bytes 221188
  86.0 9.5 %collective-permute-start.8 = (bf16[288,128]{1,0:T(8,128)(2,1)S(1)}, bf16[288,128]{1,0:T(8,128)(2,1)S(1)}, u32[]{:S(2)}, u32[]{:S(2)}) collective-permute-start(bf16[288,128]{1,0:T(8,128)(2,1)S(1)} %get-tuple-element.30), channel_id=1, source_target_pairs={{0,96},{8,104},{16,112},{24,120},{32,128},{40,136},{48,144},{56,15... | collective-permute-start | bytes 221192 | tf_op jit(solution)/shard_map/ppermute | solution.py:351
  89.6 9.5 %copy-start.12 = (bf16[288,128]{1,0:T(8,128)(2,1)}, bf16[288,128]{1,0:T(8,128)(2,1)S(1)}, u32[]{:S(2)}) copy-start(bf16[288,128]{1,0:T(8,128)(2,1)S(1)} %collective-permute-done.11.refs_6_) | copy-start | bytes 221188
  89.6 9.5 %collective-permute-start.9 = (bf16[288,128]{1,0:T(8,128)(2,1)S(1)}, bf16[288,128]{1,0:T(8,128)(2,1)S(1)}, u32[]{:S(2)}, u32[]{:S(2)}) collective-permute-start(bf16[288,128]{1,0:T(8,128)(2,1)S(1)} %get-tuple-element.31), channel_id=1, source_target_pairs={{0,128},{8,136},{16,144},{24,152},{32,160},{40,168},{48,176},{56,1... | collective-permute-start | bytes 221192 | tf_op jit(solution)/shard_map/ppermute | solution.py:351
  91.9 7.1 %copy-start.13 = (bf16[288,128]{1,0:T(8,128)(2,1)}, bf16[288,128]{1,0:T(8,128)(2,1)S(1)}, u32[]{:S(2)}) copy-start(bf16[288,128]{1,0:T(8,128)(2,1)S(1)} %collective-permute-done.12.refs_7_) | copy-start | bytes 221188
  92.0 7.1 %copy-start.14 = (bf16[288,128]{1,0:T(8,128)(2,1)}, bf16[288,128]{1,0:T(8,128)(2,1)S(1)}, u32[]{:S(2)}) copy-start(bf16[288,128]{1,0:T(8,128)(2,1)S(1)} %collective-permute-done.6.refs_1_) | copy-start | bytes 221188
  93.2 5.9 %copy-start.15 = (bf16[288,128]{1,0:T(8,128)(2,1)}, bf16[288,128]{1,0:T(8,128)(2,1)S(1)}, u32[]{:S(2)}) copy-start(bf16[288,128]{1,0:T(8,128)(2,1)S(1)} %collective-permute-done.7.refs_2_) | copy-start | bytes 221188
  95.5 3.6 %copy-start.16 = (bf16[288,128]{1,0:T(8,128)(2,1)}, bf16[288,128]{1,0:T(8,128)(2,1)S(1)}, u32[]{:S(2)}) copy-start(bf16[288,128]{1,0:T(8,128)(2,1)S(1)} %collective-permute-done.8.refs_3_) | copy-start | bytes 221188
  99.0 0.6 copy-start.17
  101.6 11.7 %copy-start.5 = (bf16[8,256,128]{2,1,0:T(8,128)(2,1)S(1)}, bf16[8,256,128]{2,1,0:T(8,128)(2,1)}, u32[]{:S(2)}) copy-start(bf16[8,256,128]{2,1,0:T(8,128)(2,1)} %get-tuple-element.35.refs_1_) | copy-start | bytes 1572868
  101.6 11.7 %copy-start.7 = (bf16[8,32,128]{2,1,0:T(8,128)(2,1)S(1)}, bf16[8,32,128]{2,1,0:T(8,128)(2,1)}, u32[]{:S(2)}) copy-start(bf16[8,32,128]{2,1,0:T(8,128)(2,1)} %get-tuple-element.36.refs_2_) | copy-start | bytes 196612
  101.6 11.7 %copy-start.9 = (s32[2]{0:T(128)S(1)}, s32[2]{0:T(128)}, u32[]{:S(2)}) copy-start(s32[2]{0:T(128)} %copy-done.8) | copy-start | bytes 28
  101.7 10.2 %collective-permute-start.13 = (bf16[8,32,128]{2,1,0:T(8,128)(2,1)}, bf16[8,32,128]{2,1,0:T(8,128)(2,1)S(1)}, u32[]{:S(2)}, u32[]{:S(2)}) collective-permute-start(bf16[8,32,128]{2,1,0:T(8,128)(2,1)} %get-tuple-element.36.refs_2_), channel_id=1, source_target_pairs={{0,8},{8,16},{16,24},{24,0},{32,40},{40,48},{48,56},{56,32},{64,72... | collective-permute-start | bytes 196616 | tf_op jit(solution)/shard_map/ppermute | solution.py:444
  101.7 10.1 %collective-permute-start.14 = (bf16[8,32,128]{2,1,0:T(8,128)(2,1)}, bf16[8,32,128]{2,1,0:T(8,128)(2,1)S(1)}, u32[]{:S(2)}, u32[]{:S(2)}) collective-permute-start(bf16[8,32,128]{2,1,0:T(8,128)(2,1)} %get-tuple-element.36.refs_2_), channel_id=1, source_target_pairs={{0,16},{8,24},{16,0},{24,8},{32,48},{40,56},{48,32},{56,40},{64,80... | collective-permute-start | bytes 196616 | tf_op jit(solution)/shard_map/ppermute | solution.py:444
  108.2 5.2 %collective-permute-start.15 = (bf16[8,32,128]{2,1,0:T(8,128)(2,1)}, bf16[8,32,128]{2,1,0:T(8,128)(2,1)S(1)}, u32[]{:S(2)}, u32[]{:S(2)}) collective-permute-start(bf16[8,32,128]{2,1,0:T(8,128)(2,1)} %get-tuple-element.36.refs_2_), channel_id=1, source_target_pairs={{0,24},{8,0},{16,8},{24,16},{32,56},{40,32},{48,40},{56,48},{64,88... | collective-permute-start | bytes 196616 | tf_op jit(solution)/shard_map/ppermute | solution.py:444
  109.7 14.9 %collective-permute-start = (bf16[8,256,128]{2,1,0:T(8,128)(2,1)S(1)}, bf16[8,256,128]{2,1,0:T(8,128)(2,1)S(1)}, u32[]{:S(2)}, u32[]{:S(2)}) collective-permute-start(bf16[8,256,128]{2,1,0:T(8,128)(2,1)S(1)} %get-tuple-element.40.k0), channel_id=1, source_target_pairs={{0,8},{8,16},{16,24},{24,0},{32,40},{40,48},{48,56},{56,32},{64,72... | collective-permute-start | bytes 1572872 | tf_op jit(solution)/shard_map/ppermute | solution.py:359
  111.8 14.9 %collective-permute-start.2 = (bf16[8,256,128]{2,1,0:T(8,128)(2,1)S(1)}, bf16[8,256,128]{2,1,0:T(8,128)(2,1)S(1)}, u32[]{:S(2)}, u32[]{:S(2)}) collective-permute-start(bf16[8,256,128]{2,1,0:T(8,128)(2,1)S(1)} %get-tuple-element.40.k0), channel_id=1, source_target_pairs={{0,24},{8,0},{16,8},{24,16},{32,56},{40,32},{48,40},{56,48},{64,88... | collective-permute-start | bytes 1572872 | tf_op jit(solution)/shard_map/ppermute | solution.py:360
  116.0 19.8 %collective-permute-start.16 = (bf16[8,256,128]{2,1,0:T(8,128)(2,1)S(1)}, bf16[8,256,128]{2,1,0:T(8,128)(2,1)S(1)}, u32[]{:S(2)}, u32[]{:S(2)}) collective-permute-start(bf16[8,256,128]{2,1,0:T(8,128)(2,1)S(1)} %values.1.v0), channel_id=1, source_target_pairs={{0,8},{8,16},{16,24},{24,0},{32,40},{40,48},{48,56},{56,32},{64,72... | collective-permute-start | bytes 1572872 | tf_op jit(solution)/shard_map/ppermute | solution.py:359
  116.6 20.9 %collective-permute-start.18 = (bf16[8,256,128]{2,1,0:T(8,128)(2,1)S(1)}, bf16[8,256,128]{2,1,0:T(8,128)(2,1)S(1)}, u32[]{:S(2)}, u32[]{:S(2)}) collective-permute-start(bf16[8,256,128]{2,1,0:T(8,128)(2,1)S(1)} %values.1.v0), channel_id=1, source_target_pairs={{0,24},{8,0},{16,8},{24,16},{32,56},{40,32},{48,40},{56,48},{64,88... | collective-permute-start | bytes 1572872 | tf_op jit(solution)/shard_map/ppermute | solution.py:360
  124.6 14.2 %collective-permute-start.1 = (bf16[4,256,128]{2,1,0:T(8,128)(2,1)S(1)}, bf16[4,256,128]{2,1,0:T(8,128)(2,1)S(1)}, u32[]{:S(2)}, u32[]{:S(2)}) collective-permute-start(bf16[4,256,128]{2,1,0:T(8,128)(2,1)S(1)} %slice.30), channel_id=1, source_target_pairs={{0,8},{8,16},{16,24},{24,0},{32,40},{40,48},{48,56},{56,32},{64,72... | collective-permute-start | bytes 786440 | tf_op jit(solution)/shard_map/ppermute | solution.py:363
  126.7 13.5 %collective-permute-start.3 = (bf16[4,256,128]{2,1,0:T(8,128)(2,1)S(1)}, bf16[4,256,128]{2,1,0:T(8,128)(2,1)S(1)}, u32[]{:S(2)}, u32[]{:S(2)}) collective-permute-start(bf16[4,256,128]{2,1,0:T(8,128)(2,1)S(1)} %slice.31), channel_id=1, source_target_pairs={{0,24},{8,0},{16,8},{24,16},{32,56},{40,32},{48,40},{56,48},{64,88... | collective-permute-start | bytes 786440 | tf_op jit(solution)/shard_map/ppermute | solution.py:364
  135.9 18.6 %collective-permute-start.17 = (bf16[4,256,128]{2,1,0:T(8,128)(2,1)S(1)}, bf16[4,256,128]{2,1,0:T(8,128)(2,1)S(1)}, u32[]{:S(2)}, u32[]{:S(2)}) collective-permute-start(bf16[4,256,128]{2,1,0:T(8,128)(2,1)S(1)} %slice.33), channel_id=1, source_target_pairs={{0,8},{8,16},{16,24},{24,0},{32,40},{40,48},{48,56},{56,32},{64,72... | collective-permute-start | bytes 786440 | tf_op jit(solution)/shard_map/ppermute | solution.py:363
  137.5 17.0 %collective-permute-start.19 = (bf16[4,256,128]{2,1,0:T(8,128)(2,1)S(1)}, bf16[4,256,128]{2,1,0:T(8,128)(2,1)S(1)}, u32[]{:S(2)}, u32[]{:S(2)}) collective-permute-start(bf16[4,256,128]{2,1,0:T(8,128)(2,1)S(1)} %slice.34), channel_id=1, source_target_pairs={{0,24},{8,0},{16,8},{24,16},{32,56},{40,32},{48,40},{56,48},{64,88... | collective-permute-start | bytes 786440 | tf_op jit(solution)/shard_map/ppermute | solution.py:364
